TPU v7x, 128 devices: a whole 4x4x4 slice. The times are simulated.
128 devices in a mesh: rep: 32 (over y, z, x_lo), grp: 4 (over x_hi, core).
Axes of the slice: x: 4 (x_hi: 2, x_lo: 2; x = x_hi * 2 + x_lo), y: 4, z: 4, core: 2. Of those that a mesh axis runs over, the one named last changes fastest.
Arguments:
- tokens: bfloat16 [64, 1024, 768], P('rep', 'grp'), may hold values from -6 to 6
- segment: int32 [64, 1024], P('rep'), may hold values from 0 to 1, as said below
- piece_start: int32 [64, 1024], P('rep'), may hold values from 0 to 1023, as said below
- w_query: bfloat16 [768, 768], P('grp'), may hold values from -0.21875 to 0.21875
- w_key: bfloat16 [768, 768], P('grp'), may hold values from -0.21875 to 0.21875
- w_value: bfloat16 [768, 768], P('grp'), may hold values from -0.21875 to 0.21875
- w_out: bfloat16 [768, 768], P('grp'), may hold values from -3.5 to 3.5
- w_gate: bfloat16 [768, 3072], P('grp'), may hold values from -0.21875 to 0.21875
- w_up: bfloat16 [768, 3072], P('grp'), may hold values from -0.21875 to 0.21875
- w_down: bfloat16 [3072, 768], P('grp'), may hold values from -0.109375 to 0.109375
- cotangent: bfloat16 [64, 1024, 768], P('rep', 'grp'), may hold values from -6 to 6
Outputs:
- output: bfloat16 [64, 1024, 768], P('rep', 'grp')
- grad_tokens: bfloat16 [64, 1024, 768], P('rep', 'grp')
- grad_query: float32 [768, 768], P('grp')
- grad_key: float32 [768, 768], P('grp')
- grad_value: float32 [768, 768], P('grp')
- grad_out: float32 [768, 768], P('grp')
- grad_gate: float32 [768, 3072], P('grp')
- grad_up: float32 [768, 3072], P('grp')
- grad_down: float32 [3072, 768], P('grp')
Inputs may be any that keep to these rules, and one draw needn't show every extreme that they name: `segment`: along a sequence the numbers start at 0, never fall, rise by one at a time, and rise only at the first position of a picture piece. `piece_start`: each sequence holds 2 picture pieces of 256 positions, the k-th lying within positions k * (512) to (k + 1) * 512 - 1; a piece's positions hold its first position, all other positions their own.
All inputs are finite; a program needn't handle non-finite values.
Results may differ from a plain program's by a relative error of at most 0.029.
Values may be sent and summed in bfloat16 or wider, within the bound.
No kernel may reach another device: no remote copies, remote signals or barrier semaphores. Data moves between devices by JAX's collectives and lax.ppermute only.
A program may use at most 256 MiB of HBM per device.

v0:
```python
import jax
import jax.numpy as jnp
from jax import lax
from jax.sharding import Mesh
from jax.sharding import PartitionSpec as P
from jax.experimental import pallas as pl
from jax.experimental.pallas import tpu as pltpu

HEADS = 12
HDIM = 64
REP = ("y", "z", "xl")
GRP = ("xh", "c")


def layer_norm(hidden):
    centred = hidden - jnp.mean(hidden, axis=-1, keepdims=True)
    spread = jnp.mean(centred * centred, axis=-1, keepdims=True)
    return centred * lax.rsqrt(spread + 1e-05)


def rotate(heads, cosine, sine):
    half = heads.shape[-1] // 2
    first = heads[..., :half]
    second = heads[..., half:]
    return jnp.concatenate(
        [first * cosine - second * sine, second * cosine + first * sine], axis=-1
    )


def gated(gate, upper):
    return gate / (1.0 + jnp.exp(-gate)) * upper


def matmul(left, right):
    return jnp.dot(left, right, preferred_element_type=jnp.float32)


def contract_rows(left, right):
    return lax.dot_general(
        left, right, (((0,), (0,)), ((), ())), preferred_element_type=jnp.float32
    )


def contract_cols(left, right):
    return lax.dot_general(
        left, right, (((1,), (1,)), ((), ())), preferred_element_type=jnp.float32
    )


def allowed_mask(rq_ref, sq_ref, pq_ref, sk_ref, pk_ref, rk_ref):
    return (sq_ref[...] == sk_ref[...]) & (
        (rk_ref[...] <= rq_ref[...]) | (pq_ref[...] == pk_ref[...])
    )


def attention_forward_kernel(
    q_ref, k_ref, v_ref, rq_ref, sq_ref, pq_ref, sk_ref, pk_ref, rk_ref, o_ref, lse_ref
):
    queries = q_ref.shape[0]
    keys = k_ref.shape[0]
    allowed = allowed_mask(rq_ref, sq_ref, pq_ref, sk_ref, pk_ref, rk_ref)
    scale = HDIM ** (-0.5)
    for h in range(q_ref.shape[1] // HDIM):
        cols = slice(h * HDIM, (h + 1) * HDIM)
        raw = lax.dot_general(
            q_ref[:, cols], k_ref[:, cols], (((1,), (1,)), ((), ())),
            preferred_element_type=jnp.float32,
        )
        scores = jnp.where(allowed, raw * scale, -1e30)
        highest = jnp.max(scores, axis=1, keepdims=True)
        expd = jnp.exp(scores - highest)
        total = jnp.sum(expd, axis=1, keepdims=True)
        probs_low = (expd / total).astype(jnp.bfloat16)
        o_ref[:, cols] = jnp.dot(probs_low, v_ref[:, cols], preferred_element_type=jnp.float32)
        lse_ref[:, h:h + 1] = highest + jnp.log(total)


def attention_backward_kernel(
    q_ref, k_ref, v_ref, do_ref, lse_ref, rq_ref, sq_ref, pq_ref, sk_ref, pk_ref, rk_ref,
    dq_ref, dk_ref, dv_ref,
):
    queries = q_ref.shape[0]
    keys = k_ref.shape[0]
    allowed = allowed_mask(rq_ref, sq_ref, pq_ref, sk_ref, pk_ref, rk_ref)
    scale = HDIM ** (-0.5)
    for h in range(q_ref.shape[1] // HDIM):
        cols = slice(h * HDIM, (h + 1) * HDIM)
        q = q_ref[:, cols]
        k = k_ref[:, cols]
        v = v_ref[:, cols]
        do = do_ref[:, cols]
        raw = lax.dot_general(q, k, (((1,), (1,)), ((), ())), preferred_element_type=jnp.float32)
        scores = jnp.where(allowed, raw * scale, -1e30)
        probs = jnp.exp(scores - lse_ref[:, h:h + 1])
        grad_probs = lax.dot_general(do, v, (((1,), (1,)), ((), ())), preferred_element_type=jnp.float32)
        inner = jnp.sum(probs * grad_probs, axis=1, keepdims=True)
        grad_raw = (probs * (grad_probs - inner) * scale).astype(jnp.bfloat16)
        dq_ref[:, cols] = jnp.dot(grad_raw, k, preferred_element_type=jnp.float32)
        dk_ref[:, cols] = lax.dot_general(
            grad_raw, q, (((0,), (0,)), ((), ())), preferred_element_type=jnp.float32
        )
        dv_ref[:, cols] = lax.dot_general(
            probs.astype(jnp.bfloat16), do, (((0,), (0,)), ((), ())), preferred_element_type=jnp.float32
        )


def mask_specs(queries, keys):
    column = pl.BlockSpec((queries, 1), lambda i: (0, 0))
    row = pl.BlockSpec((1, keys), lambda i: (0, 0))
    return [column, column, column, row, row, row]


def attention_forward(q, kv, masks):
    queries, width = q.shape
    keys = kv.shape[0]
    block = 2 * HDIM
    pairs = width // block
    return pl.pallas_call(
        attention_forward_kernel,
        grid=(pairs,),
        in_specs=[
            pl.BlockSpec((queries, block), lambda i: (0, i)),
            pl.BlockSpec((keys, block), lambda i: (0, i)),
            pl.BlockSpec((keys, block), lambda i, p=pairs: (0, i + p)),
        ] + mask_specs(queries, keys),
        out_specs=[
            pl.BlockSpec((queries, block), lambda i: (0, i)),
            pl.BlockSpec((None, queries, 2), lambda i: (i, 0, 0)),
        ],
        out_shape=[
            jax.ShapeDtypeStruct((queries, width), jnp.float32),
            jax.ShapeDtypeStruct((pairs, queries, 2), jnp.float32),
        ],
        compiler_params=pltpu.CompilerParams(dimension_semantics=("arbitrary",)),
        cost_estimate=pl.CostEstimate(
            flops=4 * queries * keys * width, transcendentals=queries * keys * HEADS,
            bytes_accessed=2 * (queries + 2 * keys) * width + 4 * queries * width,
        ),
    )(q, kv, kv, *masks)


def attention_backward(q, kv, do, lse, masks):
    queries, width = q.shape
    keys = kv.shape[0]
    block = 2 * HDIM
    pairs = width // block
    return pl.pallas_call(
        attention_backward_kernel,
        grid=(pairs,),
        in_specs=[
            pl.BlockSpec((queries, block), lambda i: (0, i)),
            pl.BlockSpec((keys, block), lambda i: (0, i)),
            pl.BlockSpec((keys, block), lambda i, p=pairs: (0, i + p)),
            pl.BlockSpec((queries, block), lambda i: (0, i)),
            pl.BlockSpec((None, queries, 2), lambda i: (i, 0, 0)),
        ] + mask_specs(queries, keys),
        out_specs=[
            pl.BlockSpec((queries, block), lambda i: (0, i)),
            pl.BlockSpec((keys, block), lambda i: (0, i)),
            pl.BlockSpec((keys, block), lambda i: (0, i)),
        ],
        out_shape=[
            jax.ShapeDtypeStruct((queries, width), jnp.float32),
            jax.ShapeDtypeStruct((keys, width), jnp.float32),
            jax.ShapeDtypeStruct((keys, width), jnp.float32),
        ],
        compiler_params=pltpu.CompilerParams(dimension_semantics=("arbitrary",)),
        cost_estimate=pl.CostEstimate(
            flops=10 * queries * keys * width, transcendentals=queries * keys * HEADS,
            bytes_accessed=2 * (2 * queries + 2 * keys) * width + 4 * (queries + 2 * keys) * width,
        ),
    )(q, kv, kv, do, lse, *masks)


def shift(x, axis, n, step):
    return lax.ppermute(x, axis, [(i, (i + step) % n) for i in range(n)])


def place(buf, piece, index, dim):
    start = [0] * buf.ndim
    start[dim] = index * piece.shape[dim]
    return lax.dynamic_update_slice(buf, piece, start)


def ring_gather(piece, axis, n, dim, direct=False):
    if n == 1:
        return piece
    me = lax.axis_index(axis)
    shape = list(piece.shape)
    shape[dim] *= n
    buf = place(jnp.zeros(shape, piece.dtype), piece, me, dim)
    if n == 2 or direct:
        for k in range(1, n):
            buf = place(buf, shift(piece, axis, n, k), (me - k) % n, dim)
        return buf
    back = piece
    ahead = piece
    for step in range(1, n // 2 + 1):
        if step < n - step:
            back = shift(back, axis, n, 1)
            ahead = shift(ahead, axis, n, -1)
            buf = place(buf, back, (me - step) % n, dim)
            buf = place(buf, ahead, (me + step) % n, dim)
        else:
            half = piece.shape[dim] // 2
            first = shift(lax.slice_in_dim(back, 0, half, axis=dim), axis, n, 1)
            second = shift(lax.slice_in_dim(ahead, half, piece.shape[dim], axis=dim), axis, n, -1)
            buf = place(buf, jnp.concatenate([first, second], axis=dim), (me + step) % n, dim)
    return buf


def ring_reduce(x, axis, n, dim, hdim, direct=False):
    if n == 1:
        return x
    me = lax.axis_index(axis)
    size = x.shape[dim] // n

    def chunk(k):
        return lax.dynamic_slice_in_dim(x, (k % n) * size, size, axis=dim)

    def low(v):
        return v.astype(jnp.bfloat16)

    if n == 2 or direct:
        acc = chunk(me)
        for k in range(1, n):
            acc = acc + shift(low(chunk(me + k)), axis, n, k).astype(jnp.float32)
        return acc
    assert n == 4
    half = x.shape[hdim] // 2

    def part(k, which):
        c = chunk(k)
        return lax.slice_in_dim(c, 0, half, axis=hdim) if which == 0 else lax.slice_in_dim(
            c, half, c.shape[hdim], axis=hdim
        )

    from_ahead = shift(low(jnp.stack([part(me - 2, 0), part(me - 1, 1)])), axis, n, -1)
    from_back = shift(low(jnp.stack([part(me + 2, 1), part(me + 1, 0)])), axis, n, 1)
    relay_ahead = shift(low(from_ahead[0].astype(jnp.float32) + part(me - 1, 0)), axis, n, -1)
    relay_back = shift(low(from_back[0].astype(jnp.float32) + part(me + 1, 1)), axis, n, 1)
    first = part(me, 0) + from_back[1].astype(jnp.float32) + relay_ahead.astype(jnp.float32)
    second = part(me, 1) + from_ahead[1].astype(jnp.float32) + relay_back.astype(jnp.float32)
    return jnp.concatenate([first, second], axis=hdim)


def cross(x):
    return lax.ppermute(x, ("xl", "xh"), [(i, 3 - i) for i in range(4)])


def swap_core(x):
    return lax.ppermute(x, "c", [(0, 1), (1, 0)])


def absolute(parts, rows):
    xh = lax.axis_index("xh")
    c = lax.axis_index("c")
    same = jnp.where(c == 0, jnp.concatenate(parts[0:2]), jnp.concatenate(parts[1::-1]))
    other = jnp.where(c == 0, jnp.concatenate(parts[2:4]), jnp.concatenate(parts[3:1:-1]))
    return jnp.where(xh == 0, jnp.concatenate([same, other]), jnp.concatenate([other, same]))


def gather_group(own, axis, n, direct):
    size = own.shape[0] // n
    me = lax.axis_index(axis)
    mine = lax.dynamic_slice_in_dim(own, me * size, size, axis=0)
    other = ring_gather(cross(mine), axis, n, 0, direct)
    partner = swap_core(jnp.concatenate([own, other]))
    rows = own.shape[0]
    return [own, partner[:rows], other, partner[rows:]]


def gather_weights(group, axis, sizes, direct):
    parts = gather_group(jnp.concatenate(group), axis, sizes[axis], direct)
    out = []
    start = 0
    for s in group:
        rows = s.shape[0]
        out.append(absolute([p[start:start + rows] for p in parts], rows))
        start += rows
    return out


def reduce_group(grads, sizes, direct):
    g = lax.axis_index("xh") * 2 + lax.axis_index("c")

    def shard(w, j):
        rows = w.shape[-2] // 4
        part = lax.dynamic_slice_in_dim(w, jnp.bitwise_xor(g, j) * rows, rows, axis=w.ndim - 2)
        return part.reshape(-1, w.shape[-1])

    send = jnp.concatenate([shard(w, 1) for w in grads] + [shard(w, 3) for w in grads])
    got = swap_core(send.astype(jnp.bfloat16))
    total = got.shape[0] // 2
    kept = jnp.stack(
        [jnp.concatenate([shard(w, 0) for w in grads]), jnp.concatenate([shard(w, 2) for w in grads])]
    )
    pair = kept.astype(jnp.float32) + got.reshape(2, total, -1).astype(jnp.float32)
    ny, nz = sizes["y"], sizes["z"]
    rows = pair.shape[1]
    own = ring_reduce(pair[0], "y", ny, 0, 1, direct)
    own = ring_reduce(own, "z", nz, 0, 1, True)
    oth = ring_reduce(pair[1].reshape(ny, rows // ny, -1), "z", nz, 1, 2, direct)
    oth = ring_reduce(oth, "y", ny, 0, 2, True).reshape(own.shape)
    low_own = own.astype(jnp.bfloat16)
    low_oth = oth.astype(jnp.bfloat16)
    mine = (
        own
        + lax.ppermute(low_own, "xl", [(0, 1), (1, 0)]).astype(jnp.float32)
        + cross(low_oth).astype(jnp.float32)
        + lax.ppermute(low_oth, "xh", [(0, 1), (1, 0)]).astype(jnp.float32)
    )
    full = ring_gather(mine.astype(jnp.bfloat16), "z", sizes["z"], 0, True)
    full = ring_gather(full, "y", sizes["y"], 0, direct)
    out = []
    start = 0
    for w in grads:
        rows = w.size // (4 * w.shape[-1])
        out.append(full[start:start + rows].astype(jnp.float32))
        start += rows
    return out


def to_sequence(x):
    xh = lax.axis_index("xh")
    c = lax.axis_index("c")
    first = lax.ppermute(lax.dynamic_index_in_dim(x, c, 0, False), GRP, [(0, 0), (1, 2), (2, 1), (3, 3)])
    second = lax.ppermute(lax.dynamic_index_in_dim(x, 1 - c, 0, False), GRP, [(0, 2), (1, 0), (2, 3), (3, 1)])
    return jnp.where(xh == 0, jnp.concatenate([first, second]), jnp.concatenate([second, first]))


def from_sequence(x):
    xh = lax.axis_index("xh")
    c = lax.axis_index("c")
    length = x.shape[0] // 2
    first = jnp.where(xh == 0, x[:length], x[length:])
    second = jnp.where(xh == 0, x[length:], x[:length])
    first = lax.ppermute(first, GRP, [(0, 0), (1, 2), (2, 1), (3, 3)])
    second = lax.ppermute(second, GRP, [(2, 0), (0, 1), (3, 2), (1, 3)])
    return jnp.where(c == 0, jnp.stack([first, second]), jnp.stack([second, first]))


def body(
    tokens, segment, piece_start, w_query, w_key, w_value, w_out, w_gate, w_up, w_down, cotangent
):
    sizes = {"y": lax.axis_size("y"), "z": lax.axis_size("z"), "xl": lax.axis_size("xl")}
    width = tokens.shape[2]
    local_length = tokens.shape[1] * 2
    full_length = segment.shape[1]
    head_count = HEADS
    head_size = HDIM
    scale = head_size ** (-0.5)
    xh = lax.axis_index("xh")
    c = lax.axis_index("c")
    first_row = c * local_length
    rows = first_row + jnp.arange(local_length, dtype=jnp.int32)
    columns = jnp.arange(full_length, dtype=jnp.int32)
    inverse = 10000.0 ** (-jnp.arange(0, head_size, 2).astype(jnp.float32) / head_size)
    angles = rows.astype(jnp.float32)[:, None] * inverse[None, :]
    cosine = jnp.cos(angles)[:, None, :]
    sine = jnp.sin(angles)[:, None, :]

    query_weight, key_weight, value_weight = gather_weights(
        (w_query, w_key, w_value), "y", sizes, True
    )

    both_in = to_sequence(jnp.concatenate([tokens, cotangent], axis=2))
    hidden = both_in[:, :width].astype(jnp.float32)
    grad_result = both_in[:, width:]
    seg_row = lax.dynamic_index_in_dim(segment, xh, 0, False)
    start_row = lax.dynamic_index_in_dim(piece_start, xh, 0, False)

    normed, norm_one_back = jax.vjp(layer_norm, hidden)
    normed_low = normed.astype(jnp.bfloat16)
    query_heads = rotate(
        matmul(normed_low, query_weight).reshape(local_length, head_count, head_size),
        cosine,
        sine,
    ).astype(jnp.bfloat16)
    keys = (
        rotate(
            matmul(normed_low, key_weight).reshape(local_length, head_count, head_size),
            cosine,
            sine,
        )
        .reshape(local_length, width)
        .astype(jnp.bfloat16)
    )
    values = matmul(normed_low, value_weight).astype(jnp.bfloat16)
    out_weight, down_weight = gather_weights((w_out, w_down), "z", sizes, False)
    gate_weight, up_weight = gather_weights((w_gate, w_up), "y", sizes, False)
    mine_kv = jnp.concatenate([keys, values], axis=1)
    both = jnp.concatenate([mine_kv, swap_core(mine_kv)])
    other_row = (1 - c) * local_length
    seg_local = lax.dynamic_slice_in_dim(seg_row, first_row, local_length)
    start_local = lax.dynamic_slice_in_dim(start_row, first_row, local_length)
    key_rows = jnp.concatenate([rows, other_row + jnp.arange(local_length, dtype=jnp.int32)])
    seg_keys = jnp.concatenate([seg_local, lax.dynamic_slice_in_dim(seg_row, other_row, local_length)])
    start_keys = jnp.concatenate(
        [start_local, lax.dynamic_slice_in_dim(start_row, other_row, local_length)]
    )
    masks = (
        rows[:, None],
        seg_local[:, None],
        start_local[:, None],
        seg_keys[None, :],
        start_keys[None, :],
        key_rows[None, :],
    )
    query_flat = query_heads.reshape(local_length, width)
    mixed, log_total = attention_forward(query_flat, both, masks)
    mixed_low = mixed.reshape(local_length, width).astype(jnp.bfloat16)
    after = hidden + matmul(mixed_low, out_weight)
    normed_two, norm_two_back = jax.vjp(layer_norm, after)
    normed_two_low = normed_two.astype(jnp.bfloat16)
    gate = matmul(normed_two_low, gate_weight)
    upper = matmul(normed_two_low, up_weight)
    active, gate_back = jax.vjp(gated, gate, upper)
    active_low = active.astype(jnp.bfloat16)
    result = after + matmul(active_low, down_weight)
    result_low = result.astype(jnp.bfloat16)

    grads = [None] * 7
    grads[6] = contract_rows(active_low, grad_result)
    grad_active = contract_cols(grad_result, down_weight)
    grad_gate, grad_upper = gate_back(grad_active)
    gate_low = grad_gate.astype(jnp.bfloat16)
    upper_low = grad_upper.astype(jnp.bfloat16)
    def blocked_grad(left, right):
        count = right.shape[1] // width
        return jnp.stack(
            [contract_rows(left, right[:, i * width:(i + 1) * width]) for i in range(count)]
        )

    grads[4] = blocked_grad(normed_two_low, gate_low)
    grads[5] = blocked_grad(normed_two_low, upper_low)
    grad_normed_two = contract_cols(gate_low, gate_weight) + contract_cols(upper_low, up_weight)
    grad_after = grad_result.astype(jnp.float32) + norm_two_back(grad_normed_two)[0]
    after_low = grad_after.astype(jnp.bfloat16)
    grads[3] = contract_rows(mixed_low, after_low)
    grad_mixed = (
        contract_cols(after_low, out_weight)
        .astype(jnp.bfloat16)
        .reshape(local_length, head_count, head_size)
    )
    grad_query, grad_keys, grad_values = attention_backward(
        query_flat, both, grad_mixed.reshape(local_length, width), log_total, masks
    )
    grad_query = grad_query.reshape(local_length, head_count, head_size)
    grad_kv = jnp.concatenate([grad_keys, grad_values], axis=1)
    own_kv = grad_kv[:local_length] + swap_core(grad_kv[local_length:])
    own_keys = own_kv[:, :width]
    own_values = own_kv[:, width:]
    query_low = (
        rotate(grad_query, cosine, -sine).reshape(local_length, width).astype(jnp.bfloat16)
    )
    keys_low = (
        rotate(own_keys.reshape(local_length, head_count, head_size), cosine, -sine)
        .reshape(local_length, width)
        .astype(jnp.bfloat16)
    )
    values_low = own_values.astype(jnp.bfloat16)
    grads[0] = contract_rows(normed_low, query_low)
    grads[1] = contract_rows(normed_low, keys_low)
    grads[2] = contract_rows(normed_low, values_low)
    grad_normed = (
        contract_cols(query_low, query_weight)
        + contract_cols(keys_low, key_weight)
        + contract_cols(values_low, value_weight)
    )
    grad_hidden = grad_after + norm_one_back(grad_normed)[0]
    both_out = from_sequence(jnp.concatenate([result_low, grad_hidden.astype(jnp.bfloat16)], axis=1))
    output = both_out[..., :width]
    input_grads = both_out[..., width:]
    blocks, gate_rows = grads[4].shape[0], grads[4].shape[1]
    low = [w.astype(jnp.bfloat16) for w in grads]
    owned = reduce_group(low, sizes, False)
    for i in (4, 5):
        owned[i] = owned[i].reshape(blocks, gate_rows // 4, width).transpose(1, 0, 2).reshape(
            gate_rows // 4, blocks * width
        )

    return (output, input_grads, *owned)


def solution(mesh):
    rep, grp = mesh.devices.shape
    side = int(round((rep // 2) ** 0.5))
    devices = mesh.devices.reshape(side, rep // (2 * side), 2, grp // 2, 2)
    fine = Mesh(devices, ("y", "z", "xl", "xh", "c"))
    seqs = P(REP, GRP, None)
    rows = P(GRP, None)
    placed = (seqs, P(REP, None), P(REP, None), rows, rows, rows, rows, rows, rows, rows, seqs)
    return jax.shard_map(
        body,
        mesh=fine,
        in_specs=placed,
        out_specs=(seqs, seqs, rows, rows, rows, rows, rows, rows, rows),
        check_vma=False,
    )
```

profile of v0, /device:TPU:0, one launch (start us, length us, event | category | flops | bytes accessed | tf_op | source)
XLA Modules:
  0.0 484.3 jit_solution(15999103917394677816)
XLA Ops:
  13.5 7.4 %collective-permute-start = (bf16[256,1536]{1,0:T(8,128)(2,1)}, bf16[256,1536]{1,0:T(8,128)(2,1)}, u32[]{:S(2)}, u32[]{:S(2)}) collective-permute-start(bf16[256,1536]{1,0:T(8,128)(2,1)} %get-tuple-element.95), channel_id=1, source_target_pairs={{0,0},{1,2},{2,1},{3,3},{4,4},{5,6},{6,5},{7,7},{8,8},{9,10},{10,9... | collective-permute-start | bytes 2359304 | tf_op jit(solution)/shard_map/ppermute | solution.py:327
  26.9 10.5 %collective-permute-done.2 = bf16[144,768]{1,0:T(8,128)(2,1)} collective-permute-done((bf16[144,768]{1,0:T(8,128)(2,1)}, bf16[144,768]{1,0:T(8,128)(2,1)}, u32[]{:S(2)}, u32[]{:S(2)}) %collective-permute-start.2) | collective-permute-done | bytes 221216 | tf_op jit(solution)/shard_map/ppermute | solution.py:248
  53.2 4.1 collective-permute-start.10
  109.6 23.8 %shard_map.178 = (f32[512,768]{1,0:T(8,128)}, f32[6,512,2]{2,1,0:T(8,128)}) custom-call(bf16[512,768]{1,0:T(8,128)(2,1)} %copy.25.q_ref, bf16[1024,1536]{1,0:T(8,128)(2,1)} %pad_maximum_fusion.3.k_ref.v_ref, bf16[1024,1536]{1,0:T(8,128)(2,1)} %pad_maximum_fusion.3.k_ref.v_ref, s32[512,1]{1,0:T(8,128)} %iota_add_fusion.rq_ref, s32[512,1]{1,0:T(8,128)} %copy.26.sq_ref, ...), custom_call_target="tpu_custom_call" | custom-call | flops 1610612736 | bytes 5505024 | tf_op jit(solution)/shard_map/pallas_call | solution.py:118
  140.5 8.1 %fusion.28 = f32[512,3072]{1,0:T(8,128)} fusion(bf16[1536,768]{1,0:T(8,128)(2,1)S(1)} %get-tuple-element.138, bf16[1536,768]{1,0:T(8,128)(2,1)S(1)} %get-tuple-element.137, pred[]{:T(512)S(6)} %eq.70, bf16[512,1536]{1,0:T(8,128)(2,1)S(1)} %maximum_select_fusion.7), kind=kOutput, calls=%fused_computation.142 | convolution fusion | flops 2437152768 | bytes 11796481 | tf_op jit(solution)/shard_map/dot_general | solution.py:45
  156.5 4.7 fusion.31
  161.3 12.5 %multiply_convert_fusion.1 = (bf16[512,3072]{1,0:T(8,128)(2,1)}, bf16[512,3072]{1,0:T(8,128)(2,1)}, bf16[512,3072]{1,0:T(8,128)(2,1)}) fusion(f32[512,3072]{1,0:T(8,128)} %fusion.31, f32[512,3072]{1,0:T(8,128)} %fusion.28, bf16[512,768]{1,0:T(8,128)(2,1)S(1)} %multiply_convert_fusion.2, bf16[384,3072]{1,0:T(8,128)(2,1)S(1)} %get-tuple-element.136, ...), kind=kOutput, calls=%fused_computation.4 | convolution fusion | flops 2465464320 | bytes 27525120 | tf_op jit(solution)/shard_map/dot_general | solution.py:35
  190.2 30.9 %shard_map.179 = (f32[512,768]{1,0:T(8,128)}, f32[1024,768]{1,0:T(8,128)}, f32[1024,768]{1,0:T(8,128)}) custom-call(bf16[512,768]{1,0:T(8,128)(2,1)} %copy.25.q_ref, bf16[1024,1536]{1,0:T(8,128)(2,1)} %pad_maximum_fusion.3.k_ref.v_ref, bf16[1024,1536]{1,0:T(8,128)(2,1)} %pad_maximum_fusion.3.k_ref.v_ref, bf16[512,768]{1,0:T(8,128)(2,1)} %convolution_convert_fusion.13.do_ref, ...), custom_call_target="tpu_custom_call" | custom-call | flops 4026531840 | bytes 12582912 | tf_op jit(solution)/shard_map/pallas_call | solution.py:147
  249.7 4.8 convolution_convert_fusion
  290.5 8.2 %add_convert_fusion.2 = bf16[512,768]{1,0:T(8,128)(2,1)} fusion(f32[512,768]{1,0:T(8,128)S(1)} %get-tuple-element.124, bf16[512,3072]{1,0:T(8,128)(2,1)} %get-tuple-element.27, bf16[1536,768]{1,0:T(8,128)(2,1)} %copy-done.39, bf16[1536,768]{1,0:T(8,128)(2,1)} %copy-done.38, pred[]{:T(512)S(6)} %eq.70), kind=kOutput, calls=%fused_computation.72 | convolution fusion | flops 2437939200 | bytes 10223617 | tf_op jit(solution)/shard_map/dot_general | solution.py:35
  298.7 6.5 %collective-permute-done.23 = bf16[6144,768]{1,0:T(8,128)(2,1)} collective-permute-done((bf16[6144,768]{1,0:T(8,128)(2,1)}, bf16[6144,768]{1,0:T(8,128)(2,1)}, u32[]{:S(2)}, u32[]{:S(2)}) %collective-permute-start.23) | collective-permute-done | bytes 9437216 | tf_op jit(solution)/shard_map/ppermute | solution.py:252
  305.2 7.3 %convert_add_fusion = f32[2,3072,768]{2,1,0:T(8,128)S(1)} fusion(bf16[2,3072,768]{2,1,0:T(8,128)(2,1)} %bitcast.67, bf16[1,3072,768]{2,1,0:T(8,128)(2,1)} %bitcast.34, bf16[1,3072,768]{2,1,0:T(8,128)(2,1)} %bitcast.31), kind=kLoop, calls=%fused_computation | loop fusion | flops 18874368 | bytes 37748736 | tf_op jit(solution)/shard_map/add | solution.py:298
  312.5 7.1 %fusion.109 = (f32[1,3072,768]{2,1,0:T(8,128)}, f32[1,3072,768]{2,1,0:T(8,128)}) fusion(f32[2,3072,768]{2,1,0:T(8,128)S(1)} %convert_add_fusion), kind=kLoop, calls=%fused_computation.328 | loop fusion | bytes 37748736 | tf_op jit(solution)/shard_map/slice | solution.py:301
  337.3 14.8 %collective-permute-done.32 = bf16[2,4,192,384]{3,2,1,0:T(8,128)(2,1)S(1)} collective-permute-done((bf16[2,4,192,384]{3,2,1,0:T(8,128)(2,1)S(1)}, bf16[2,4,192,384]{3,2,1,0:T(8,128)(2,1)S(1)}, u32[]{:S(2)}, u32[]{:S(2)}) %collective-permute-start.32) | collective-permute-done | bytes 1179680 | tf_op jit(solution)/shard_map/ppermute | solution.py:176
  353.2 5.8 %collective-permute-done.24 = bf16[2,768,384]{2,1,0:T(8,128)(2,1)S(1)} collective-permute-done((bf16[2,768,384]{2,1,0:T(8,128)(2,1)S(1)}, bf16[2,768,384]{2,1,0:T(8,128)(2,1)S(1)}, u32[]{:S(2)}, u32[]{:S(2)}) %collective-permute-start.24) | collective-permute-done | bytes 1179680 | tf_op jit(solution)/shard_map/ppermute | solution.py:176
  362.7 5.5 %collective-permute-done.35 = bf16[4,192,384]{2,1,0:T(8,128)(2,1)S(1)} collective-permute-done((bf16[4,192,384]{2,1,0:T(8,128)(2,1)S(1)}, bf16[4,192,384]{2,1,0:T(8,128)(2,1)S(1)}, u32[]{:S(2)}, u32[]{:S(2)}) %collective-permute-start.35) | collective-permute-done | bytes 589856 | tf_op jit(solution)/shard_map/ppermute | solution.py:176
  369.9 5.6 %collective-permute-done.27 = bf16[768,384]{1,0:T(8,128)(2,1)S(1)} collective-permute-done((bf16[768,384]{1,0:T(8,128)(2,1)S(1)}, bf16[768,384]{1,0:T(8,128)(2,1)S(1)}, u32[]{:S(2)}, u32[]{:S(2)}) %collective-permute-start.27) | collective-permute-done | bytes 589856 | tf_op jit(solution)/shard_map/ppermute | solution.py:176
  379.5 5.5 %collective-permute-done.34 = bf16[4,192,384]{2,1,0:T(8,128)(2,1)S(1)} collective-permute-done((bf16[4,192,384]{2,1,0:T(8,128)(2,1)S(1)}, bf16[4,192,384]{2,1,0:T(8,128)(2,1)S(1)}, u32[]{:S(2)}, u32[]{:S(2)}) %collective-permute-start.34) | collective-permute-done | bytes 589856 | tf_op jit(solution)/shard_map/ppermute | solution.py:176
  405.3 5.4 %collective-permute-done.40 = bf16[192,768]{1,0:T(8,128)(2,1)S(1)} collective-permute-done((bf16[192,768]{1,0:T(8,128)(2,1)S(1)}, bf16[192,768]{1,0:T(8,128)(2,1)S(1)}, u32[]{:S(2)}, u32[]{:S(2)}) %collective-permute-start.40) | collective-permute-done | bytes 294944 | tf_op jit(solution)/shard_map/ppermute | solution.py:311
  418.5 6.6 %collective-permute-done.41 = bf16[192,768]{1,0:T(8,128)(2,1)S(1)} collective-permute-done((bf16[192,768]{1,0:T(8,128)(2,1)S(1)}, bf16[192,768]{1,0:T(8,128)(2,1)S(1)}, u32[]{:S(2)}, u32[]{:S(2)}) %collective-permute-start.41) | collective-permute-done | bytes 294944 | tf_op jit(solution)/shard_map/ppermute | solution.py:176
  434.5 7.4 %collective-permute-start.21 = (bf16[256,1536]{1,0:T(8,128)(2,1)}, bf16[256,1536]{1,0:T(8,128)(2,1)}, u32[]{:S(2)}, u32[]{:S(2)}) collective-permute-start(bf16[256,1536]{1,0:T(8,128)(2,1)} %get-tuple-element.93), channel_id=1, source_target_pairs={{0,0},{1,2},{2,1},{3,3},{4,4},{5,6},{6,5},{7,7},{8,8},{9,10},{10,9... | collective-permute-start | bytes 2359304 | tf_op jit(solution)/shard_map/ppermute | solution.py:338
  441.9 6.4 %collective-permute-done.22 = bf16[256,1536]{1,0:T(8,128)(2,1)} collective-permute-done((bf16[256,1536]{1,0:T(8,128)(2,1)}, bf16[256,1536]{1,0:T(8,128)(2,1)}, u32[]{:S(2)}, u32[]{:S(2)}) %collective-permute-start.22) | collective-permute-done | bytes 786464 | tf_op jit(solution)/shard_map/ppermute | solution.py:339
  450.4 8.1 %collective-permute-done.45 = bf16[768,768]{1,0:T(8,128)(2,1)S(1)} collective-permute-done((bf16[768,768]{1,0:T(8,128)(2,1)S(1)}, bf16[768,768]{1,0:T(8,128)(2,1)S(1)}, u32[]{:S(2)}, u32[]{:S(2)}) %collective-permute-start.45) | collective-permute-done | bytes 1179680 | tf_op jit(solution)/shard_map/ppermute | solution.py:176
  462.7 11.4 %collective-permute-done.47 = bf16[384,768]{1,0:T(8,128)(2,1)S(1)} collective-permute-done((bf16[384,768]{1,0:T(8,128)(2,1)S(1)}, bf16[384,768]{1,0:T(8,128)(2,1)S(1)}, u32[]{:S(2)}, u32[]{:S(2)}) %collective-permute-start.47) | collective-permute-done | bytes 589856 | tf_op jit(solution)/shard_map/ppermute | solution.py:176
  (434 shorter events, 263.6 us)
Async XLA Ops:
  2.7 37.3 %collective-permute-start.8 = (bf16[240,768]{1,0:T(8,128)(2,1)}, bf16[240,768]{1,0:T(8,128)(2,1)}, u32[]{:S(2)}, u32[]{:S(2)}) collective-permute-start(bf16[240,768]{1,0:T(8,128)(2,1)} %fusion.73), channel_id=1, source_target_pairs={{0,6},{2,4},{4,2},{6,0},{1,7},{3,5},{5,3},{7,1},{8,14},{10,12},{12... | collective-permute-start | bytes 1105928 | tf_op jit(solution)/shard_map/ppermute | solution.py:248
  6.6 30.7 %collective-permute-start.2 = (bf16[144,768]{1,0:T(8,128)(2,1)}, bf16[144,768]{1,0:T(8,128)(2,1)}, u32[]{:S(2)}, u32[]{:S(2)}) collective-permute-start(bf16[144,768]{1,0:T(8,128)(2,1)} %fusion.76), channel_id=1, source_target_pairs={{0,6},{2,4},{4,2},{6,0},{1,7},{3,5},{5,3},{7,1},{8,14},{10,12},{12... | collective-permute-start | bytes 663560 | tf_op jit(solution)/shard_map/ppermute | solution.py:248
  11.6 54.5 %collective-permute-start.1 = (bf16[256,1536]{1,0:T(8,128)(2,1)}, bf16[256,1536]{1,0:T(8,128)(2,1)}, u32[]{:S(2)}, u32[]{:S(2)}) collective-permute-start(bf16[256,1536]{1,0:T(8,128)(2,1)} %get-tuple-element.96), channel_id=1, source_target_pairs={{0,2},{1,0},{2,3},{3,1},{4,6},{5,4},{6,7},{7,5},{8,10},{9,8},{10,1... | collective-permute-start | bytes 2359304 | tf_op jit(solution)/shard_map/ppermute | solution.py:328
  13.5 56.3 %collective-permute-start = (bf16[256,1536]{1,0:T(8,128)(2,1)}, bf16[256,1536]{1,0:T(8,128)(2,1)}, u32[]{:S(2)}, u32[]{:S(2)}) collective-permute-start(bf16[256,1536]{1,0:T(8,128)(2,1)} %get-tuple-element.95), channel_id=1, source_target_pairs={{0,0},{1,2},{2,1},{3,3},{4,4},{5,6},{6,5},{7,7},{8,8},{9,10},{10,9... | collective-permute-start | bytes 2359304 | tf_op jit(solution)/shard_map/ppermute | solution.py:327
  22.1 35.5 %collective-permute-start.14 = (bf16[96,3072]{1,0:T(8,128)(2,1)}, bf16[96,3072]{1,0:T(8,128)(2,1)}, u32[]{:S(2)}, u32[]{:S(2)}) collective-permute-start(bf16[96,3072]{1,0:T(8,128)(2,1)} %fusion.47), channel_id=1, source_target_pairs={{0,6},{2,4},{4,2},{6,0},{1,7},{3,5},{5,3},{7,1},{8,14},{10,12},{12... | collective-permute-start | bytes 1769480 | tf_op jit(solution)/shard_map/ppermute | solution.py:248
  57.5 26.8 %collective-permute-start.6 = (bf16[1152,768]{1,0:T(8,128)(2,1)S(1)}, bf16[1152,768]{1,0:T(8,128)(2,1)S(1)}, u32[]{:S(2)}, u32[]{:S(2)}) collective-permute-start(bf16[1152,768]{1,0:T(8,128)(2,1)S(1)} %pad_maximum_fusion.7), channel_id=1, source_target_pairs={{0,1},{1,0},{2,3},{3,2},{4,5},{5,4},{6,7},{7,6},{8,9},{9,8},{10,11... | collective-permute-start | bytes 5308424 | tf_op jit(solution)/shard_map/ppermute | solution.py:252
  62.7 20.6 %collective-permute-start.15 = (bf16[96,3072]{1,0:T(8,128)(2,1)}, bf16[96,3072]{1,0:T(8,128)(2,1)S(1)}, u32[]{:S(2)}, u32[]{:S(2)}) collective-permute-start(bf16[96,3072]{1,0:T(8,128)(2,1)} %collective-permute-done.14), channel_id=1, source_target_pairs={{0,32},{32,64},{64,96},{96,0},{1,33},{33,65},{65,97},{97,1},{2,34}... | collective-permute-start | bytes 1769480 | tf_op jit(solution)/shard_map/ppermute | solution.py:176
  80.2 53.2 %collective-permute-start.13 = (bf16[1920,768]{1,0:T(8,128)(2,1)}, bf16[1920,768]{1,0:T(8,128)(2,1)}, u32[]{:S(2)}, u32[]{:S(2)}) collective-permute-start(bf16[1920,768]{1,0:T(8,128)(2,1)} %pad_maximum_fusion.4), channel_id=1, source_target_pairs={{0,1},{1,0},{2,3},{3,2},{4,5},{5,4},{6,7},{7,6},{8,9},{9,8},{10,11... | collective-permute-start | bytes 8847368 | tf_op jit(solution)/shard_map/ppermute | solution.py:252
  80.9 16.7 %collective-permute-start.18 = (bf16[48,3072]{1,0:T(8,128)(2,1)}, bf16[48,3072]{1,0:T(8,128)(2,1)}, u32[]{:S(2)}, u32[]{:S(2)}) collective-permute-start(bf16[48,3072]{1,0:T(8,128)(2,1)} %slice.395), channel_id=1, source_target_pairs={{0,96},{32,0},{64,32},{96,64},{1,97},{33,1},{65,33},{97,65},{2,98}... | collective-permute-start | bytes 884744 | tf_op jit(solution)/shard_map/ppermute | solution.py:176
  101.1 47.4 %collective-permute-start.19 = (bf16[768,3072]{1,0:T(8,128)(2,1)}, bf16[768,3072]{1,0:T(8,128)(2,1)}, u32[]{:S(2)}, u32[]{:S(2)}) collective-permute-start(bf16[768,3072]{1,0:T(8,128)(2,1)} %pad_maximum_fusion), channel_id=1, source_target_pairs={{0,1},{1,0},{2,3},{3,2},{4,5},{5,4},{6,7},{7,6},{8,9},{9,8},{10,11... | collective-permute-start | bytes 14155784 | tf_op jit(solution)/shard_map/ppermute | solution.py:252
  228.1 26.4 %collective-permute-start.20 = (f32[512,1536]{1,0:T(8,128)}, f32[512,1536]{1,0:T(8,128)}, u32[]{:S(2)}, u32[]{:S(2)}) collective-permute-start(f32[512,1536]{1,0:T(8,128)} %slice.409), channel_id=1, source_target_pairs={{0,1},{1,0},{2,3},{3,2},{4,5},{5,4},{6,7},{7,6},{8,9},{9,8},{10,11... | collective-permute-start | bytes 9437192 | tf_op jit(solution)/shard_map/ppermute | solution.py:252
  322.5 29.6 %collective-permute-start.32 = (bf16[2,4,192,384]{3,2,1,0:T(8,128)(2,1)S(1)}, bf16[2,4,192,384]{3,2,1,0:T(8,128)(2,1)S(1)}, u32[]{:S(2)}, u32[]{:S(2)}) collective-permute-start(bf16[2,4,192,384]{3,2,1,0:T(8,128)(2,1)S(1)} %pad_maximum_fusion.11), channel_id=1, source_target_pairs={{0,8},{8,16},{16,24},{24,0},{1,9},{9,17},{17,25},{25,1},{2,10},{10... | collective-permute-start | bytes 3538952 | tf_op jit(solution)/shard_map/ppermute | solution.py:176
  329.3 29.7 %collective-permute-start.24 = (bf16[2,768,384]{2,1,0:T(8,128)(2,1)S(1)}, bf16[2,768,384]{2,1,0:T(8,128)(2,1)S(1)}, u32[]{:S(2)}, u32[]{:S(2)}) collective-permute-start(bf16[2,768,384]{2,1,0:T(8,128)(2,1)S(1)} %pad_maximum_fusion.9), channel_id=1, source_target_pairs={{0,32},{32,64},{64,96},{96,0},{1,33},{33,65},{65,97},{97,1},{2,34}... | collective-permute-start | bytes 3538952 | tf_op jit(solution)/shard_map/ppermute | solution.py:176
  331.1 28.2 %collective-permute-start.25 = (bf16[2,768,384]{2,1,0:T(8,128)(2,1)S(1)}, bf16[2,768,384]{2,1,0:T(8,128)(2,1)S(1)}, u32[]{:S(2)}, u32[]{:S(2)}) collective-permute-start(bf16[2,768,384]{2,1,0:T(8,128)(2,1)S(1)} %pad_maximum_fusion.10), channel_id=1, source_target_pairs={{0,96},{32,0},{64,32},{96,64},{1,97},{33,1},{65,33},{97,65},{2,98}... | collective-permute-start | bytes 3538952 | tf_op jit(solution)/shard_map/ppermute | solution.py:176
  333.2 29.6 %collective-permute-start.33 = (bf16[2,4,192,384]{3,2,1,0:T(8,128)(2,1)S(1)}, bf16[2,4,192,384]{3,2,1,0:T(8,128)(2,1)S(1)}, u32[]{:S(2)}, u32[]{:S(2)}) collective-permute-start(bf16[2,4,192,384]{3,2,1,0:T(8,128)(2,1)S(1)} %pad_maximum_fusion.12), channel_id=1, source_target_pairs={{0,24},{8,0},{16,8},{24,16},{1,25},{9,1},{17,9},{25,17},{2,26},{10... | collective-permute-start | bytes 3538952 | tf_op jit(solution)/shard_map/ppermute | solution.py:176
  352.3 16.0 %collective-permute-start.35 = (bf16[4,192,384]{2,1,0:T(8,128)(2,1)S(1)}, bf16[4,192,384]{2,1,0:T(8,128)(2,1)S(1)}, u32[]{:S(2)}, u32[]{:S(2)}) collective-permute-start(bf16[4,192,384]{2,1,0:T(8,128)(2,1)S(1)} %fusion.19), channel_id=1, source_target_pairs={{0,8},{8,16},{16,24},{24,0},{1,9},{9,17},{17,25},{25,1},{2,10},{10... | collective-permute-start | bytes 1769480 | tf_op jit(solution)/shard_map/ppermute | solution.py:176
  359.2 16.3 %collective-permute-start.27 = (bf16[768,384]{1,0:T(8,128)(2,1)S(1)}, bf16[768,384]{1,0:T(8,128)(2,1)S(1)}, u32[]{:S(2)}, u32[]{:S(2)}) collective-permute-start(bf16[768,384]{1,0:T(8,128)(2,1)S(1)} %fusion.23), channel_id=1, source_target_pairs={{0,32},{32,64},{64,96},{96,0},{1,33},{33,65},{65,97},{97,1},{2,34}... | collective-permute-start | bytes 1769480 | tf_op jit(solution)/shard_map/ppermute | solution.py:176
  359.5 15.9 %collective-permute-start.26 = (bf16[768,384]{1,0:T(8,128)(2,1)S(1)}, bf16[768,384]{1,0:T(8,128)(2,1)S(1)}, u32[]{:S(2)}, u32[]{:S(2)}) collective-permute-start(bf16[768,384]{1,0:T(8,128)(2,1)S(1)} %fusion.25), channel_id=1, source_target_pairs={{0,96},{32,0},{64,32},{96,64},{1,97},{33,1},{65,33},{97,65},{2,98}... | collective-permute-start | bytes 1769480 | tf_op jit(solution)/shard_map/ppermute | solution.py:176
  368.7 16.3 %collective-permute-start.34 = (bf16[4,192,384]{2,1,0:T(8,128)(2,1)S(1)}, bf16[4,192,384]{2,1,0:T(8,128)(2,1)S(1)}, u32[]{:S(2)}, u32[]{:S(2)}) collective-permute-start(bf16[4,192,384]{2,1,0:T(8,128)(2,1)S(1)} %get-tuple-element.31), channel_id=1, source_target_pairs={{0,24},{8,0},{16,8},{24,16},{1,25},{9,1},{17,9},{25,17},{2,26},{10... | collective-permute-start | bytes 1769480 | tf_op jit(solution)/shard_map/ppermute | solution.py:176
  375.9 15.4 %collective-permute-start.30 = (bf16[192,768]{1,0:T(8,128)(2,1)S(1)}, bf16[192,768]{1,0:T(8,128)(2,1)S(1)}, u32[]{:S(2)}, u32[]{:S(2)}) collective-permute-start(bf16[192,768]{1,0:T(8,128)(2,1)S(1)} %get-tuple-element.69), channel_id=1, source_target_pairs={{0,24},{8,0},{16,8},{24,16},{1,25},{9,1},{17,9},{25,17},{2,26},{10... | collective-permute-start | bytes 884744 | tf_op jit(solution)/shard_map/ppermute | solution.py:176
  428.4 32.2 %collective-permute-start.44 = (bf16[768,768]{1,0:T(8,128)(2,1)S(1)}, bf16[768,768]{1,0:T(8,128)(2,1)S(1)}, u32[]{:S(2)}, u32[]{:S(2)}) collective-permute-start(bf16[768,768]{1,0:T(8,128)(2,1)S(1)} %constant_dynamic-update-slice_fusion.15), channel_id=1, source_target_pairs={{0,32},{32,64},{64,96},{96,0},{1,33},{33,65},{65,97},{97,1},{2,34}... | collective-permute-start | bytes 3538952 | tf_op jit(solution)/shard_map/ppermute | solution.py:176
  430.9 27.6 %collective-permute-start.45 = (bf16[768,768]{1,0:T(8,128)(2,1)S(1)}, bf16[768,768]{1,0:T(8,128)(2,1)S(1)}, u32[]{:S(2)}, u32[]{:S(2)}) collective-permute-start(bf16[768,768]{1,0:T(8,128)(2,1)S(1)} %constant_dynamic-update-slice_fusion.15), channel_id=1, source_target_pairs={{0,96},{32,0},{64,32},{96,64},{1,97},{33,1},{65,33},{97,65},{2,98}... | collective-permute-start | bytes 3538952 | tf_op jit(solution)/shard_map/ppermute | solution.py:176
  458.5 15.5 %collective-permute-start.47 = (bf16[384,768]{1,0:T(8,128)(2,1)S(1)}, bf16[384,768]{1,0:T(8,128)(2,1)S(1)}, u32[]{:S(2)}, u32[]{:S(2)}) collective-permute-start(bf16[384,768]{1,0:T(8,128)(2,1)S(1)} %slice.445), channel_id=1, source_target_pairs={{0,96},{32,0},{64,32},{96,64},{1,97},{33,1},{65,33},{97,65},{2,98}... | collective-permute-start | bytes 1769480 | tf_op jit(solution)/shard_map/ppermute | solution.py:176
  460.6 16.4 %collective-permute-start.46 = (bf16[384,768]{1,0:T(8,128)(2,1)S(1)}, bf16[384,768]{1,0:T(8,128)(2,1)S(1)}, u32[]{:S(2)}, u32[]{:S(2)}) collective-permute-start(bf16[384,768]{1,0:T(8,128)(2,1)S(1)} %slice.444), channel_id=1, source_target_pairs={{0,32},{32,64},{64,96},{96,0},{1,33},{33,65},{65,97},{97,1},{2,34}... | collective-permute-start | bytes 1769480 | tf_op jit(solution)/shard_map/ppermute | solution.py:176
  (112 other events, 1091.0 us)
where the time goes:
time: 493 us; the launch traced here: 484 us
  waiting for transfers between devices  125 us (25%)
  local copies, waits for them, and re-layouts  94 us (19%)
  starting transfers between devices  75.8 us (15%)
  matrix products  72 us (15%)
  other arithmetic  60.1 us (12%)
  Pallas kernels  54.7 us (11%)
    ppermute x32, waiting for transfers between devices, shift(): return lax.ppermute(x, axis, [(i, (i + step) % n) for i in range(n)])  93.3 us
    ppermute x32, starting transfers between devices, shift(): return lax.ppermute(x, axis, [(i, (i + step) % n) for i in range(n)])  51 us
    unnamed x195, local copies, waits for them, and re-layouts  31.3 us
    pallas_call x1, Pallas kernels, attention_backward(): pl.pallas_call(attention_backward_kernel, grid=(pairs,), in_specs=[pl.Blo...  30.9 us
    dot_general x7, matrix products, matmul(): return jnp.dot(left, right, preferred_element_type=jnp.float32)  30.1 us
    pallas_call x1, Pallas kernels, attention_forward(): pl.pallas_call(attention_forward_kernel, grid=(pairs,), in_specs=[pl.Bloc...  23.8 us
    dot_general x13, matrix products, contract_rows(): lax.dot_general(left, right, (((0,), (0,)), ((), ())), preferred_element_...  23.7 us
    dot_general x7, matrix products, contract_cols(): lax.dot_general(left, right, (((1,), (1,)), ((), ())), preferred_element_...  18.2 us
  transfers between devices with their start and end apart: 48, of which 27 were waited for; matrix products, arithmetic and copies ran while one was open for 23% of the time, Pallas kernels for 5%

commit v1 on v0

--- a/solution.py
+++ b/solution.py
@@ -284,18 +284,19 @@
 def reduce_group(grads, sizes, direct):
     g = lax.axis_index("xh") * 2 + lax.axis_index("c")
 
-    def shard(w, j):
-        rows = w.shape[-2] // 4
-        part = lax.dynamic_slice_in_dim(w, jnp.bitwise_xor(g, j) * rows, rows, axis=w.ndim - 2)
-        return part.reshape(-1, w.shape[-1])
-
-    send = jnp.concatenate([shard(w, 1) for w in grads] + [shard(w, 3) for w in grads])
-    got = swap_core(send.astype(jnp.bfloat16))
-    total = got.shape[0] // 2
-    kept = jnp.stack(
-        [jnp.concatenate([shard(w, 0) for w in grads]), jnp.concatenate([shard(w, 2) for w in grads])]
-    )
-    pair = kept.astype(jnp.float32) + got.reshape(2, total, -1).astype(jnp.float32)
+    def by_shard(w):
+        if w.ndim == 2:
+            return w.reshape(4, -1, w.shape[-1])
+        blocks, rows, width = w.shape
+        return w.reshape(blocks, 4, rows // 4, width).transpose(1, 0, 2, 3).reshape(4, -1, width)
+
+    every = jnp.concatenate([by_shard(w) for w in grads], axis=1)
+
+    def shard(j):
+        return lax.dynamic_index_in_dim(every, jnp.bitwise_xor(g, j), 0, False)
+
+    got = swap_core(jnp.stack([shard(1), shard(3)]))
+    pair = jnp.stack([shard(0), shard(2)]).astype(jnp.float32) + got.astype(jnp.float32)
     ny, nz = sizes["y"], sizes["z"]
     rows = pair.shape[1]
     own = ring_reduce(pair[0], "y", ny, 0, 1, direct)

time: 493 us -> 481 us (0.976)
  local copies, waits for them, and re-layouts: 94 us -> 77.7 us
  other arithmetic: 60.1 us -> 69.2 us
  waiting for transfers between devices: 125 us -> 120 us
    unnamed x195 -> x174, local copies, waits for them, and re-layouts: 31.3 us -> 14.2 us
    ppermute x32, waiting for transfers between devices: 93.3 us -> 79.1 us  [shift(): return lax.ppermute(x, axis, [(i, (i + step) % n) for i in range(n)])]
    ppermute x1, waiting for transfers between devices: 6.36 us -> 15.6 us  [from_sequence(): second = lax.ppermute(second, GRP, [(2, 0), (0, 1), (3, 2), (1, 3)])]
    ppermute x1, starting transfers between devices: 7.44 us -> 1.78 us  [to_sequence(): lax.ppermute(lax.dynamic_index_in_dim(x, c, 0, False), GRP, [(0, 0), (1,...]
    transpose x0 -> x2, local copies, waits for them, and re-layouts: none -> 5.18 us  [by_shard(): w.reshape(blocks, 4, rows // 4, width).transpose(1, 0, 2, 3)]
    another operation x4 -> x3, other arithmetic: 7.23 us -> 12.2 us  [the longest x1 8.4 us: reduce_group(): got = swap_core(jnp.stack([shard(1), shard(3)]))]
  transfers between devices with their start and end apart: 48 -> 48, of which waited for: 27 -> 19; matrix products, arithmetic and copies ran while one was open for 23% -> 22% of each run, Pallas kernels for 5% -> 5%
where the time goes in v1:
time: 481 us; the launch traced here: 472 us
  waiting for transfers between devices  120 us (25%)
  local copies, waits for them, and re-layouts  77.7 us (16%)
  starting transfers between devices  75.6 us (16%)
  matrix products  72.3 us (15%)
  other arithmetic  69.2 us (14%)
  Pallas kernels  54.7 us (11%)
    ppermute x32, waiting for transfers between devices, shift(): return lax.ppermute(x, axis, [(i, (i + step) % n) for i in range(n)])  79.1 us
    ppermute x32, starting transfers between devices, shift(): return lax.ppermute(x, axis, [(i, (i + step) % n) for i in range(n)])  53.4 us
    pallas_call x1, Pallas kernels, attention_backward(): pl.pallas_call(attention_backward_kernel, grid=(pairs,), in_specs=[pl.Blo...  31 us
    dot_general x7, matrix products, matmul(): return jnp.dot(left, right, preferred_element_type=jnp.float32)  30.1 us
    dot_general x13, matrix products, contract_rows(): lax.dot_general(left, right, (((0,), (0,)), ((), ())), preferred_element_...  24.2 us
    pallas_call x1, Pallas kernels, attention_forward(): pl.pallas_call(attention_forward_kernel, grid=(pairs,), in_specs=[pl.Bloc...  23.6 us
    dot_general x7, matrix products, contract_cols(): lax.dot_general(left, right, (((1,), (1,)), ((), ())), preferred_element_...  18.1 us
    ppermute x1, waiting for transfers between devices, from_sequence(): second = lax.ppermute(second, GRP, [(2, 0), (0, 1), (3, 2), (1, 3)])  15.6 us
  transfers between devices with their start and end apart: 48, of which 19 were waited for; matrix products, arithmetic and copies ran while one was open for 22% of the time, Pallas kernels for 5%

profile of v1, /device:TPU:0, one launch (start us, length us, event | category | flops | bytes accessed | tf_op | source)
XLA Modules:
  0.0 472.3 jit_solution(16833785302817547647)
XLA Ops:
  28.3 9.0 %collective-permute-done.8 = bf16[240,768]{1,0:T(8,128)(2,1)} collective-permute-done((bf16[240,768]{1,0:T(8,128)(2,1)}, bf16[240,768]{1,0:T(8,128)(2,1)}, u32[]{:S(2)}, u32[]{:S(2)}) %collective-permute-start.8) | collective-permute-done | bytes 368672 | tf_op jit(solution)/shard_map/ppermute | solution.py:248
  103.3 23.6 %shard_map.178 = (f32[512,768]{1,0:T(8,128)}, f32[6,512,2]{2,1,0:T(8,128)}) custom-call(bf16[512,768]{1,0:T(8,128)(2,1)} %copy.27.q_ref, bf16[1024,1536]{1,0:T(8,128)(2,1)} %pad_maximum_fusion.2.k_ref.v_ref, bf16[1024,1536]{1,0:T(8,128)(2,1)} %pad_maximum_fusion.2.k_ref.v_ref, s32[512,1]{1,0:T(8,128)} %iota_add_fusion.rq_ref, s32[512,1]{1,0:T(8,128)} %copy.28.sq_ref, ...), custom_call_target="tpu_custom_call" | custom-call | flops 1610612736 | bytes 5505024 | tf_op jit(solution)/shard_map/pallas_call | solution.py:118
  134.0 8.0 %fusion.20 = f32[512,3072]{1,0:T(8,128)} fusion(bf16[1536,768]{1,0:T(8,128)(2,1)S(1)} %get-tuple-element.119, bf16[1536,768]{1,0:T(8,128)(2,1)S(1)} %get-tuple-element.118, pred[]{:T(512)S(6)} %eq.70, bf16[512,1536]{1,0:T(8,128)(2,1)S(1)} %maximum_select_fusion.7), kind=kOutput, calls=%fused_computation.131 | convolution fusion | flops 2437152768 | bytes 11796481 | tf_op jit(solution)/shard_map/dot_general | solution.py:45
  151.7 4.7 fusion.23
  156.4 12.4 %multiply_convert_fusion.1 = (bf16[512,3072]{1,0:T(8,128)(2,1)}, bf16[512,3072]{1,0:T(8,128)(2,1)}, bf16[512,3072]{1,0:T(8,128)(2,1)}) fusion(f32[512,3072]{1,0:T(8,128)} %fusion.23, f32[512,3072]{1,0:T(8,128)} %fusion.20, bf16[512,768]{1,0:T(8,128)(2,1)S(1)} %multiply_convert_fusion.2, bf16[384,3072]{1,0:T(8,128)(2,1)S(1)} %copy-done.31, ...), kind=kOutput, calls=%fused_computation.5 | convolution fusion | flops 2465464320 | bytes 27525120 | tf_op jit(solution)/shard_map/dot_general | solution.py:35
  186.1 31.0 %shard_map.179 = (f32[512,768]{1,0:T(8,128)}, f32[1024,768]{1,0:T(8,128)}, f32[1024,768]{1,0:T(8,128)}) custom-call(bf16[512,768]{1,0:T(8,128)(2,1)} %copy.27.q_ref, bf16[1024,1536]{1,0:T(8,128)(2,1)} %pad_maximum_fusion.2.k_ref.v_ref, bf16[1024,1536]{1,0:T(8,128)(2,1)} %pad_maximum_fusion.2.k_ref.v_ref, bf16[512,768]{1,0:T(8,128)(2,1)} %convolution_convert_fusion.13.do_ref, ...), custom_call_target="tpu_custom_call" | custom-call | flops 4026531840 | bytes 12582912 | tf_op jit(solution)/shard_map/pallas_call | solution.py:147
  239.8 4.5 convolution_convert_fusion
  260.8 6.5 %constant_dynamic-slice_fusion.3 = (bf16[1,3072,768]{2,1,0:T(8,128)(2,1)}, bf16[1,3072,768]{2,1,0:T(8,128)(2,1)}, bf16[1,3072,768]{2,1,0:T(8,128)(2,1)}, bf16[1,3072,768]{2,1,0:T(8,128)(2,1)}) fusion(bf16[4,3072,768]{2,1,0:T(8,128)(2,1)S(1)} %constant_dynamic-update-slice_fusion.4, s32[]{:T(128)S(6)} %select_n.453, s32[]{:T(128)S(6)} %select_n.456, ...), kind=kLoop, calls=%fused_computation.251 | loop fusion | bytes 37748752 | tf_op jit(solution)/shard_map/jit(dynamic_index_in_dim)/dynamic_slice | solution.py:296
  267.4 8.4 %pad_maximum_fusion = bf16[2,3072,768]{2,1,0:T(8,128)(2,1)} fusion(bf16[1,3072,768]{2,1,0:T(8,128)(2,1)} %get-tuple-element.28, bf16[1,3072,768]{2,1,0:T(8,128)(2,1)} %get-tuple-element.29), kind=kLoop, calls=%fused_computation.1 | loop fusion | flops 4718592 | bytes 18874368 | tf_op jit(solution)/shard_map/stack | solution.py:298
  276.0 8.2 %add_convert_fusion.2 = bf16[512,768]{1,0:T(8,128)(2,1)} fusion(f32[512,768]{1,0:T(8,128)S(1)} %copy-done.5, bf16[512,3072]{1,0:T(8,128)(2,1)} %get-tuple-element.31, bf16[1536,768]{1,0:T(8,128)(2,1)} %copy-done.27, bf16[1536,768]{1,0:T(8,128)(2,1)} %copy-done.26, pred[]{:T(512)S(6)} %eq.70), kind=kOutput, calls=%fused_computation.73 | convolution fusion | flops 2437939200 | bytes 10223617 | tf_op jit(solution)/shard_map/dot_general | solution.py:35
  284.2 6.6 %collective-permute-done.23 = bf16[2,3072,768]{2,1,0:T(8,128)(2,1)} collective-permute-done((bf16[2,3072,768]{2,1,0:T(8,128)(2,1)}, bf16[2,3072,768]{2,1,0:T(8,128)(2,1)}, u32[]{:S(2)}, u32[]{:S(2)}) %collective-permute-start.23) | collective-permute-done | bytes 9437216 | tf_op jit(solution)/shard_map/ppermute | solution.py:252
  290.8 7.5 %convert_add_fusion = f32[2,3072,768]{2,1,0:T(8,128)S(1)} fusion(bf16[2,3072,768]{2,1,0:T(8,128)(2,1)} %collective-permute-done.23, bf16[1,3072,768]{2,1,0:T(8,128)(2,1)} %get-tuple-element.30, bf16[1,3072,768]{2,1,0:T(8,128)(2,1)} %get-tuple-element.27), kind=kLoop, calls=%fused_computation | loop fusion | flops 18874368 | bytes 37748736 | tf_op jit(solution)/shard_map/add | solution.py:299
  298.2 7.0 %fusion.101 = (f32[1,3072,768]{2,1,0:T(8,128)}, f32[1,3072,768]{2,1,0:T(8,128)}) fusion(f32[2,3072,768]{2,1,0:T(8,128)S(1)} %convert_add_fusion), kind=kLoop, calls=%fused_computation.296 | loop fusion | bytes 37748736 | tf_op jit(solution)/shard_map/slice | solution.py:302
  321.5 21.2 %collective-permute-done.32 = bf16[2,4,192,384]{3,2,1,0:T(8,128)(2,1)S(1)} collective-permute-done((bf16[2,4,192,384]{3,2,1,0:T(8,128)(2,1)S(1)}, bf16[2,4,192,384]{3,2,1,0:T(8,128)(2,1)S(1)}, u32[]{:S(2)}, u32[]{:S(2)}) %collective-permute-start.32) | collective-permute-done | bytes 1179680 | tf_op jit(solution)/shard_map/ppermute | solution.py:176
  347.4 11.4 %collective-permute-done.35 = bf16[4,192,384]{2,1,0:T(8,128)(2,1)S(1)} collective-permute-done((bf16[4,192,384]{2,1,0:T(8,128)(2,1)S(1)}, bf16[4,192,384]{2,1,0:T(8,128)(2,1)S(1)}, u32[]{:S(2)}, u32[]{:S(2)}) %collective-permute-start.35) | collective-permute-done | bytes 589856 | tf_op jit(solution)/shard_map/ppermute | solution.py:176
  363.3 4.4 collective-permute-start.29
  367.7 9.6 %collective-permute-done.34 = bf16[4,192,384]{2,1,0:T(8,128)(2,1)S(1)} collective-permute-done((bf16[4,192,384]{2,1,0:T(8,128)(2,1)S(1)}, bf16[4,192,384]{2,1,0:T(8,128)(2,1)S(1)}, u32[]{:S(2)}, u32[]{:S(2)}) %collective-permute-start.34) | collective-permute-done | bytes 589856 | tf_op jit(solution)/shard_map/ppermute | solution.py:176
  377.7 4.5 collective-permute-start.37
  395.5 5.4 %collective-permute-done.40 = bf16[192,768]{1,0:T(8,128)(2,1)S(1)} collective-permute-done((bf16[192,768]{1,0:T(8,128)(2,1)S(1)}, bf16[192,768]{1,0:T(8,128)(2,1)S(1)}, u32[]{:S(2)}, u32[]{:S(2)}) %collective-permute-start.40) | collective-permute-done | bytes 294944 | tf_op jit(solution)/shard_map/ppermute | solution.py:312
  408.9 6.6 %collective-permute-done.41 = bf16[192,768]{1,0:T(8,128)(2,1)S(1)} collective-permute-done((bf16[192,768]{1,0:T(8,128)(2,1)S(1)}, bf16[192,768]{1,0:T(8,128)(2,1)S(1)}, u32[]{:S(2)}, u32[]{:S(2)}) %collective-permute-start.41) | collective-permute-done | bytes 294944 | tf_op jit(solution)/shard_map/ppermute | solution.py:176
  415.6 5.6 %collective-permute-start.45 = (bf16[768,768]{1,0:T(8,128)(2,1)S(1)}, bf16[768,768]{1,0:T(8,128)(2,1)S(1)}, u32[]{:S(2)}, u32[]{:S(2)}) collective-permute-start(bf16[768,768]{1,0:T(8,128)(2,1)S(1)} %constant_dynamic-update-slice_fusion.14), channel_id=1, source_target_pairs={{0,96},{32,0},{64,32},{96,64},{1,97},{33,1},{65,33},{97,65},{2,98}... | collective-permute-start | bytes 3538952 | tf_op jit(solution)/shard_map/ppermute | solution.py:176
  422.6 7.4 %collective-permute-start.21 = (bf16[256,1536]{1,0:T(8,128)(2,1)}, bf16[256,1536]{1,0:T(8,128)(2,1)}, u32[]{:S(2)}, u32[]{:S(2)}) collective-permute-start(bf16[256,1536]{1,0:T(8,128)(2,1)} %get-tuple-element.86), channel_id=1, source_target_pairs={{0,0},{1,2},{2,1},{3,3},{4,4},{5,6},{6,5},{7,7},{8,8},{9,10},{10,9... | collective-permute-start | bytes 2359304 | tf_op jit(solution)/shard_map/ppermute | solution.py:339
  430.0 15.6 %collective-permute-done.22 = bf16[256,1536]{1,0:T(8,128)(2,1)} collective-permute-done((bf16[256,1536]{1,0:T(8,128)(2,1)}, bf16[256,1536]{1,0:T(8,128)(2,1)}, u32[]{:S(2)}, u32[]{:S(2)}) %collective-permute-start.22) | collective-permute-done | bytes 786464 | tf_op jit(solution)/shard_map/ppermute | solution.py:340
  452.8 8.6 %collective-permute-done.47 = bf16[384,768]{1,0:T(8,128)(2,1)S(1)} collective-permute-done((bf16[384,768]{1,0:T(8,128)(2,1)S(1)}, bf16[384,768]{1,0:T(8,128)(2,1)S(1)}, u32[]{:S(2)}, u32[]{:S(2)}) %collective-permute-start.47) | collective-permute-done | bytes 589856 | tf_op jit(solution)/shard_map/ppermute | solution.py:176
  (415 shorter events, 232.0 us)
Async XLA Ops:
  2.6 23.0 %collective-permute-start.2 = (bf16[144,768]{1,0:T(8,128)(2,1)}, bf16[144,768]{1,0:T(8,128)(2,1)}, u32[]{:S(2)}, u32[]{:S(2)}) collective-permute-start(bf16[144,768]{1,0:T(8,128)(2,1)} %fusion.68), channel_id=1, source_target_pairs={{0,6},{2,4},{4,2},{6,0},{1,7},{3,5},{5,3},{7,1},{8,14},{10,12},{12... | collective-permute-start | bytes 663560 | tf_op jit(solution)/shard_map/ppermute | solution.py:248
  7.4 29.9 %collective-permute-start.8 = (bf16[240,768]{1,0:T(8,128)(2,1)}, bf16[240,768]{1,0:T(8,128)(2,1)}, u32[]{:S(2)}, u32[]{:S(2)}) collective-permute-start(bf16[240,768]{1,0:T(8,128)(2,1)} %fusion.65), channel_id=1, source_target_pairs={{0,6},{2,4},{4,2},{6,0},{1,7},{3,5},{5,3},{7,1},{8,14},{10,12},{12... | collective-permute-start | bytes 1105928 | tf_op jit(solution)/shard_map/ppermute | solution.py:248
  8.9 41.1 %collective-permute-start.14 = (bf16[96,3072]{1,0:T(8,128)(2,1)}, bf16[96,3072]{1,0:T(8,128)(2,1)}, u32[]{:S(2)}, u32[]{:S(2)}) collective-permute-start(bf16[96,3072]{1,0:T(8,128)(2,1)} %fusion.39), channel_id=1, source_target_pairs={{0,6},{2,4},{4,2},{6,0},{1,7},{3,5},{5,3},{7,1},{8,14},{10,12},{12... | collective-permute-start | bytes 1769480 | tf_op jit(solution)/shard_map/ppermute | solution.py:248
  14.0 45.7 %collective-permute-start = (bf16[256,1536]{1,0:T(8,128)(2,1)}, bf16[256,1536]{1,0:T(8,128)(2,1)S(1)}, u32[]{:S(2)}, u32[]{:S(2)}) collective-permute-start(bf16[256,1536]{1,0:T(8,128)(2,1)} %get-tuple-element.88), channel_id=1, source_target_pairs={{0,0},{1,2},{2,1},{3,3},{4,4},{5,6},{6,5},{7,7},{8,8},{9,10},{10,9... | collective-permute-start | bytes 2359304 | tf_op jit(solution)/shard_map/ppermute | solution.py:328
  15.8 45.5 %collective-permute-start.1 = (bf16[256,1536]{1,0:T(8,128)(2,1)S(1)}, bf16[256,1536]{1,0:T(8,128)(2,1)S(1)}, u32[]{:S(2)}, u32[]{:S(2)}) collective-permute-start(bf16[256,1536]{1,0:T(8,128)(2,1)S(1)} %get-tuple-element.89), channel_id=1, source_target_pairs={{0,2},{1,0},{2,3},{3,1},{4,6},{5,4},{6,7},{7,5},{8,10},{9,8},{10,1... | collective-permute-start | bytes 2359304 | tf_op jit(solution)/shard_map/ppermute | solution.py:329
  25.7 16.0 %collective-permute-start.3 = (bf16[144,768]{1,0:T(8,128)(2,1)}, bf16[144,768]{1,0:T(8,128)(2,1)S(1)}, u32[]{:S(2)}, u32[]{:S(2)}) collective-permute-start(bf16[144,768]{1,0:T(8,128)(2,1)} %collective-permute-done.2), channel_id=1, source_target_pairs={{0,32},{32,64},{64,96},{96,0},{1,33},{33,65},{65,97},{97,1},{2,34}... | collective-permute-start | bytes 663560 | tf_op jit(solution)/shard_map/ppermute | solution.py:176
  50.0 27.9 %collective-permute-start.6 = (bf16[1152,768]{1,0:T(8,128)(2,1)S(1)}, bf16[1152,768]{1,0:T(8,128)(2,1)S(1)}, u32[]{:S(2)}, u32[]{:S(2)}) collective-permute-start(bf16[1152,768]{1,0:T(8,128)(2,1)S(1)} %pad_maximum_fusion.6), channel_id=1, source_target_pairs={{0,1},{1,0},{2,3},{3,2},{4,5},{5,4},{6,7},{7,6},{8,9},{9,8},{10,11... | collective-permute-start | bytes 5308424 | tf_op jit(solution)/shard_map/ppermute | solution.py:252
  54.3 18.3 %collective-permute-start.16 = (bf16[96,3072]{1,0:T(8,128)(2,1)}, bf16[96,3072]{1,0:T(8,128)(2,1)S(1)}, u32[]{:S(2)}, u32[]{:S(2)}) collective-permute-start(bf16[96,3072]{1,0:T(8,128)(2,1)} %collective-permute-done.14), channel_id=1, source_target_pairs={{0,96},{32,0},{64,32},{96,64},{1,97},{33,1},{65,33},{97,65},{2,98}... | collective-permute-start | bytes 1769480 | tf_op jit(solution)/shard_map/ppermute | solution.py:176
  58.0 18.6 %collective-permute-start.15 = (bf16[96,3072]{1,0:T(8,128)(2,1)}, bf16[96,3072]{1,0:T(8,128)(2,1)S(1)}, u32[]{:S(2)}, u32[]{:S(2)}) collective-permute-start(bf16[96,3072]{1,0:T(8,128)(2,1)} %collective-permute-done.14), channel_id=1, source_target_pairs={{0,32},{32,64},{64,96},{96,0},{1,33},{33,65},{65,97},{97,1},{2,34}... | collective-permute-start | bytes 1769480 | tf_op jit(solution)/shard_map/ppermute | solution.py:176
  72.6 54.3 %collective-permute-start.13 = (bf16[1920,768]{1,0:T(8,128)(2,1)}, bf16[1920,768]{1,0:T(8,128)(2,1)}, u32[]{:S(2)}, u32[]{:S(2)}) collective-permute-start(bf16[1920,768]{1,0:T(8,128)(2,1)} %pad_maximum_fusion.3), channel_id=1, source_target_pairs={{0,1},{1,0},{2,3},{3,2},{4,5},{5,4},{6,7},{7,6},{8,9},{9,8},{10,11... | collective-permute-start | bytes 8847368 | tf_op jit(solution)/shard_map/ppermute | solution.py:252
  73.4 17.8 %collective-permute-start.18 = (bf16[48,3072]{1,0:T(8,128)(2,1)}, bf16[48,3072]{1,0:T(8,128)(2,1)}, u32[]{:S(2)}, u32[]{:S(2)}) collective-permute-start(bf16[48,3072]{1,0:T(8,128)(2,1)} %slice.395), channel_id=1, source_target_pairs={{0,96},{32,0},{64,32},{96,64},{1,97},{33,1},{65,33},{97,65},{2,98}... | collective-permute-start | bytes 884744 | tf_op jit(solution)/shard_map/ppermute | solution.py:176
  94.7 47.3 %collective-permute-start.19 = (bf16[768,3072]{1,0:T(8,128)(2,1)}, bf16[768,3072]{1,0:T(8,128)(2,1)}, u32[]{:S(2)}, u32[]{:S(2)}) collective-permute-start(bf16[768,3072]{1,0:T(8,128)(2,1)} %pad_maximum_fusion.1), channel_id=1, source_target_pairs={{0,1},{1,0},{2,3},{3,2},{4,5},{5,4},{6,7},{7,6},{8,9},{9,8},{10,11... | collective-permute-start | bytes 14155784 | tf_op jit(solution)/shard_map/ppermute | solution.py:252
  223.7 20.6 %collective-permute-start.20 = (f32[512,1536]{1,0:T(8,128)S(1)}, f32[512,1536]{1,0:T(8,128)S(1)}, u32[]{:S(2)}, u32[]{:S(2)}) collective-permute-start(f32[512,1536]{1,0:T(8,128)S(1)} %slice.409), channel_id=1, source_target_pairs={{0,1},{1,0},{2,3},{3,2},{4,5},{5,4},{6,7},{7,6},{8,9},{9,8},{10,11... | collective-permute-start | bytes 9437192 | tf_op jit(solution)/shard_map/ppermute | solution.py:252
  313.3 29.4 %collective-permute-start.32 = (bf16[2,4,192,384]{3,2,1,0:T(8,128)(2,1)S(1)}, bf16[2,4,192,384]{3,2,1,0:T(8,128)(2,1)S(1)}, u32[]{:S(2)}, u32[]{:S(2)}) collective-permute-start(bf16[2,4,192,384]{3,2,1,0:T(8,128)(2,1)S(1)} %pad_maximum_fusion.10), channel_id=1, source_target_pairs={{0,8},{8,16},{16,24},{24,0},{1,9},{9,17},{17,25},{25,1},{2,10},{10... | collective-permute-start | bytes 3538952 | tf_op jit(solution)/shard_map/ppermute | solution.py:176
  313.5 30.3 %collective-permute-start.25 = (bf16[2,768,384]{2,1,0:T(8,128)(2,1)S(1)}, bf16[2,768,384]{2,1,0:T(8,128)(2,1)S(1)}, u32[]{:S(2)}, u32[]{:S(2)}) collective-permute-start(bf16[2,768,384]{2,1,0:T(8,128)(2,1)S(1)} %pad_maximum_fusion.9), channel_id=1, source_target_pairs={{0,96},{32,0},{64,32},{96,64},{1,97},{33,1},{65,33},{97,65},{2,98}... | collective-permute-start | bytes 3538952 | tf_op jit(solution)/shard_map/ppermute | solution.py:176
  317.1 30.0 %collective-permute-start.24 = (bf16[2,768,384]{2,1,0:T(8,128)(2,1)S(1)}, bf16[2,768,384]{2,1,0:T(8,128)(2,1)S(1)}, u32[]{:S(2)}, u32[]{:S(2)}) collective-permute-start(bf16[2,768,384]{2,1,0:T(8,128)(2,1)S(1)} %pad_maximum_fusion.8), channel_id=1, source_target_pairs={{0,32},{32,64},{64,96},{96,0},{1,33},{33,65},{65,97},{97,1},{2,34}... | collective-permute-start | bytes 3538952 | tf_op jit(solution)/shard_map/ppermute | solution.py:176
  317.4 30.0 %collective-permute-start.33 = (bf16[2,4,192,384]{3,2,1,0:T(8,128)(2,1)S(1)}, bf16[2,4,192,384]{3,2,1,0:T(8,128)(2,1)S(1)}, u32[]{:S(2)}, u32[]{:S(2)}) collective-permute-start(bf16[2,4,192,384]{3,2,1,0:T(8,128)(2,1)S(1)} %pad_maximum_fusion.11), channel_id=1, source_target_pairs={{0,24},{8,0},{16,8},{24,16},{1,25},{9,1},{17,9},{25,17},{2,26},{10... | collective-permute-start | bytes 3538952 | tf_op jit(solution)/shard_map/ppermute | solution.py:176
  343.9 16.4 %collective-permute-start.26 = (bf16[768,384]{1,0:T(8,128)(2,1)S(1)}, bf16[768,384]{1,0:T(8,128)(2,1)S(1)}, u32[]{:S(2)}, u32[]{:S(2)}) collective-permute-start(bf16[768,384]{1,0:T(8,128)(2,1)S(1)} %fusion.17), channel_id=1, source_target_pairs={{0,96},{32,0},{64,32},{96,64},{1,97},{33,1},{65,33},{97,65},{2,98}... | collective-permute-start | bytes 1769480 | tf_op jit(solution)/shard_map/ppermute | solution.py:176
  359.1 18.2 %collective-permute-start.34 = (bf16[4,192,384]{2,1,0:T(8,128)(2,1)S(1)}, bf16[4,192,384]{2,1,0:T(8,128)(2,1)S(1)}, u32[]{:S(2)}, u32[]{:S(2)}) collective-permute-start(bf16[4,192,384]{2,1,0:T(8,128)(2,1)S(1)} %get-tuple-element.35), channel_id=1, source_target_pairs={{0,24},{8,0},{16,8},{24,16},{1,25},{9,1},{17,9},{25,17},{2,26},{10... | collective-permute-start | bytes 1769480 | tf_op jit(solution)/shard_map/ppermute | solution.py:176
  363.3 18.9 %collective-permute-start.28 = (bf16[192,768]{1,0:T(8,128)(2,1)S(1)}, bf16[192,768]{1,0:T(8,128)(2,1)S(1)}, u32[]{:S(2)}, u32[]{:S(2)}) collective-permute-start(bf16[192,768]{1,0:T(8,128)(2,1)S(1)} %get-tuple-element.60), channel_id=1, source_target_pairs={{0,8},{8,16},{16,24},{24,0},{1,9},{9,17},{17,25},{25,1},{2,10},{10... | collective-permute-start | bytes 884744 | tf_op jit(solution)/shard_map/ppermute | solution.py:176
  363.3 19.1 %collective-permute-start.29 = (bf16[192,768]{1,0:T(8,128)(2,1)S(1)}, bf16[192,768]{1,0:T(8,128)(2,1)S(1)}, u32[]{:S(2)}, u32[]{:S(2)}) collective-permute-start(bf16[192,768]{1,0:T(8,128)(2,1)S(1)} %get-tuple-element.61), channel_id=1, source_target_pairs={{0,16},{8,24},{16,0},{24,8},{1,17},{9,25},{17,1},{25,9},{2,18},{10... | collective-permute-start | bytes 884744 | tf_op jit(solution)/shard_map/ppermute | solution.py:176
  367.7 17.9 %collective-permute-start.30 = (bf16[192,768]{1,0:T(8,128)(2,1)S(1)}, bf16[192,768]{1,0:T(8,128)(2,1)S(1)}, u32[]{:S(2)}, u32[]{:S(2)}) collective-permute-start(bf16[192,768]{1,0:T(8,128)(2,1)S(1)} %get-tuple-element.62), channel_id=1, source_target_pairs={{0,24},{8,0},{16,8},{24,16},{1,25},{9,1},{17,9},{25,17},{2,26},{10... | collective-permute-start | bytes 884744 | tf_op jit(solution)/shard_map/ppermute | solution.py:176
  415.6 32.1 %collective-permute-start.45 = (bf16[768,768]{1,0:T(8,128)(2,1)S(1)}, bf16[768,768]{1,0:T(8,128)(2,1)S(1)}, u32[]{:S(2)}, u32[]{:S(2)}) collective-permute-start(bf16[768,768]{1,0:T(8,128)(2,1)S(1)} %constant_dynamic-update-slice_fusion.14), channel_id=1, source_target_pairs={{0,96},{32,0},{64,32},{96,64},{1,97},{33,1},{65,33},{97,65},{2,98}... | collective-permute-start | bytes 3538952 | tf_op jit(solution)/shard_map/ppermute | solution.py:176
  421.1 29.6 %collective-permute-start.44 = (bf16[768,768]{1,0:T(8,128)(2,1)S(1)}, bf16[768,768]{1,0:T(8,128)(2,1)S(1)}, u32[]{:S(2)}, u32[]{:S(2)}) collective-permute-start(bf16[768,768]{1,0:T(8,128)(2,1)S(1)} %constant_dynamic-update-slice_fusion.14), channel_id=1, source_target_pairs={{0,32},{32,64},{64,96},{96,0},{1,33},{33,65},{65,97},{97,1},{2,34}... | collective-permute-start | bytes 3538952 | tf_op jit(solution)/shard_map/ppermute | solution.py:176
  (107 other events, 1011.1 us)

commit v2 on v1

--- a/solution.py
+++ b/solution.py
@@ -186,27 +186,27 @@
     if n == 1:
         return piece
     me = lax.axis_index(axis)
-    shape = list(piece.shape)
-    shape[dim] *= n
-    buf = place(jnp.zeros(shape, piece.dtype), piece, me, dim)
+    by_offset = [piece] + [None] * (n - 1)
     if n == 2 or direct:
         for k in range(1, n):
-            buf = place(buf, shift(piece, axis, n, k), (me - k) % n, dim)
-        return buf
-    back = piece
-    ahead = piece
-    for step in range(1, n // 2 + 1):
-        if step < n - step:
-            back = shift(back, axis, n, 1)
-            ahead = shift(ahead, axis, n, -1)
-            buf = place(buf, back, (me - step) % n, dim)
-            buf = place(buf, ahead, (me + step) % n, dim)
-        else:
-            half = piece.shape[dim] // 2
-            first = shift(lax.slice_in_dim(back, 0, half, axis=dim), axis, n, 1)
-            second = shift(lax.slice_in_dim(ahead, half, piece.shape[dim], axis=dim), axis, n, -1)
-            buf = place(buf, jnp.concatenate([first, second], axis=dim), (me + step) % n, dim)
-    return buf
+            by_offset[(-k) % n] = shift(piece, axis, n, k)
+    else:
+        back = piece
+        ahead = piece
+        for step in range(1, n // 2 + 1):
+            if step < n - step:
+                back = shift(back, axis, n, 1)
+                ahead = shift(ahead, axis, n, -1)
+                by_offset[(-step) % n] = back
+                by_offset[step % n] = ahead
+            else:
+                half = piece.shape[dim] // 2
+                first = shift(lax.slice_in_dim(back, 0, half, axis=dim), axis, n, 1)
+                second = shift(lax.slice_in_dim(ahead, half, piece.shape[dim], axis=dim), axis, n, -1)
+                by_offset[step % n] = jnp.concatenate([first, second], axis=dim)
+    doubled = jnp.concatenate(by_offset + by_offset, axis=dim)
+    size = piece.shape[dim]
+    return lax.dynamic_slice_in_dim(doubled, ((n - me) % n) * size, n * size, axis=dim)
 
 
 def ring_reduce(x, axis, n, dim, hdim, direct=False):

time: 481 us -> 501 us (1.042)
  local copies, waits for them, and re-layouts: 77.7 us -> 97 us
    unnamed x174 -> x230, local copies, waits for them, and re-layouts: 14.2 us -> 33.5 us
    ppermute x1, waiting for transfers between devices: 15.6 us -> 0.01 us  [from_sequence(): second = lax.ppermute(second, GRP, [(2, 0), (0, 1), (3, 2), (1, 3)])]
    ppermute x6, waiting for transfers between devices: 6.6 us -> 14.6 us  [swap_core(): return lax.ppermute(x, 'c', [(0, 1), (1, 0)])]
    slice x8, local copies, waits for them, and re-layouts: 9.63 us -> 15.2 us  [gather_weights(): out.append(absolute([p[start:start + rows] for p in parts], rows))]
  transfers between devices with their start and end apart: 48 -> 48, of which waited for: 19 -> 24; matrix products, arithmetic and copies ran while one was open for 22% -> 22% of each run, Pallas kernels for 5% -> 5%
where the time goes in v2:
time: 501 us; the launch traced here: 492 us
  waiting for transfers between devices  117 us (23%)
  local copies, waits for them, and re-layouts  97 us (19%)
  starting transfers between devices  78.6 us (16%)
  other arithmetic  72.3 us (14%)
  matrix products  69.9 us (14%)
  Pallas kernels  54.8 us (11%)
    ppermute x32, waiting for transfers between devices, shift(): return lax.ppermute(x, axis, [(i, (i + step) % n) for i in range(n)])  82.8 us
    ppermute x32, starting transfers between devices, shift(): return lax.ppermute(x, axis, [(i, (i + step) % n) for i in range(n)])  54.4 us
    unnamed x230, local copies, waits for them, and re-layouts  33.5 us
    pallas_call x1, Pallas kernels, attention_backward(): pl.pallas_call(attention_backward_kernel, grid=(pairs,), in_specs=[pl.Blo...  30.9 us
    dot_general x7, matrix products, matmul(): return jnp.dot(left, right, preferred_element_type=jnp.float32)  27.5 us
    dot_general x13, matrix products, contract_rows(): lax.dot_general(left, right, (((0,), (0,)), ((), ())), preferred_element_...  24.5 us
    pallas_call x1, Pallas kernels, attention_forward(): pl.pallas_call(attention_forward_kernel, grid=(pairs,), in_specs=[pl.Bloc...  23.9 us
    dot_general x7, matrix products, contract_cols(): lax.dot_general(left, right, (((1,), (1,)), ((), ())), preferred_element_...  18 us
  transfers between devices with their start and end apart: 48, of which 24 were waited for; matrix products, arithmetic and copies ran while one was open for 22% of the time, Pallas kernels for 5%

profile of v2, /device:TPU:0, one launch (start us, length us, event | category | flops | bytes accessed | tf_op | source)
XLA Modules:
  0.0 492.0 jit_solution(11318116567162014356)
XLA Ops:
  27.2 9.1 %collective-permute-done.8 = bf16[240,768]{1,0:T(8,128)(2,1)} collective-permute-done((bf16[240,768]{1,0:T(8,128)(2,1)}, bf16[240,768]{1,0:T(8,128)(2,1)}, u32[]{:S(2)}, u32[]{:S(2)}) %collective-permute-start.8) | collective-permute-done | bytes 368672 | tf_op jit(solution)/shard_map/ppermute | solution.py:248
  47.9 4.0 collective-permute-start.9
  74.8 7.0 %collective-permute-done.17 = bf16[48,3072]{1,0:T(8,128)(2,1)S(1)} collective-permute-done((bf16[48,3072]{1,0:T(8,128)(2,1)S(1)}, bf16[48,3072]{1,0:T(8,128)(2,1)S(1)}, u32[]{:S(2)}, u32[]{:S(2)}) %collective-permute-start.17) | collective-permute-done | bytes 294944 | tf_op jit(solution)/shard_map/ppermute | solution.py:176
  116.1 23.9 %shard_map.178 = (f32[512,768]{1,0:T(8,128)}, f32[6,512,2]{2,1,0:T(8,128)}) custom-call(bf16[512,768]{1,0:T(8,128)(2,1)} %copy.27.q_ref, bf16[1024,1536]{1,0:T(8,128)(2,1)} %pad_maximum_fusion.2.k_ref.v_ref, bf16[1024,1536]{1,0:T(8,128)(2,1)} %pad_maximum_fusion.2.k_ref.v_ref, s32[512,1]{1,0:T(8,128)} %iota_add_fusion.rq_ref, s32[512,1]{1,0:T(8,128)} %copy.28.sq_ref, ...), custom_call_target="tpu_custom_call" | custom-call | flops 1610612736 | bytes 5505024 | tf_op jit(solution)/shard_map/pallas_call | solution.py:118
  147.0 7.9 %fusion.20 = f32[512,3072]{1,0:T(8,128)} fusion(bf16[1536,768]{1,0:T(8,128)(2,1)S(1)} %get-tuple-element.121, bf16[1536,768]{1,0:T(8,128)(2,1)S(1)} %get-tuple-element.120, pred[]{:T(512)S(6)} %eq.60, bf16[512,1536]{1,0:T(8,128)(2,1)S(1)} %maximum_select_fusion.7), kind=kOutput, calls=%fused_computation.130 | convolution fusion | flops 2437152768 | bytes 11796481 | tf_op jit(solution)/shard_map/dot_general | solution.py:45
  164.7 4.7 fusion.23
  169.4 12.4 %multiply_convert_fusion.1 = (bf16[512,3072]{1,0:T(8,128)(2,1)}, bf16[512,3072]{1,0:T(8,128)(2,1)}, bf16[512,3072]{1,0:T(8,128)(2,1)}) fusion(f32[512,3072]{1,0:T(8,128)} %fusion.23, f32[512,3072]{1,0:T(8,128)} %fusion.20, bf16[512,768]{1,0:T(8,128)(2,1)S(1)} %multiply_convert_fusion.2, bf16[384,3072]{1,0:T(8,128)(2,1)S(1)} %copy-done.35, ...), kind=kOutput, calls=%fused_computation.5 | convolution fusion | flops 2465464320 | bytes 27525120 | tf_op jit(solution)/shard_map/dot_general | solution.py:35
  199.1 30.9 %shard_map.179 = (f32[512,768]{1,0:T(8,128)}, f32[1024,768]{1,0:T(8,128)}, f32[1024,768]{1,0:T(8,128)}) custom-call(bf16[512,768]{1,0:T(8,128)(2,1)} %copy.27.q_ref, bf16[1024,1536]{1,0:T(8,128)(2,1)} %pad_maximum_fusion.2.k_ref.v_ref, bf16[1024,1536]{1,0:T(8,128)(2,1)} %pad_maximum_fusion.2.k_ref.v_ref, bf16[512,768]{1,0:T(8,128)(2,1)} %convolution_convert_fusion.13.do_ref, ...), custom_call_target="tpu_custom_call" | custom-call | flops 4026531840 | bytes 12582912 | tf_op jit(solution)/shard_map/pallas_call | solution.py:147
  252.6 4.8 convolution_convert_fusion
  273.8 6.7 %constant_dynamic-slice_fusion.13 = (bf16[1,3072,768]{2,1,0:T(8,128)(2,1)}, bf16[1,3072,768]{2,1,0:T(8,128)(2,1)}, bf16[1,3072,768]{2,1,0:T(8,128)(2,1)}, bf16[1,3072,768]{2,1,0:T(8,128)(2,1)}) fusion(bf16[4,3072,768]{2,1,0:T(8,128)(2,1)S(1)} %constant_dynamic-update-slice_fusion.32, s32[]{:T(128)S(6)} %select_n.392, s32[]{:T(128)S(6)} %select_n.395, ...), kind=kLoop, calls=%fused_computation.297 | loop fusion | bytes 37748752 | tf_op jit(solution)/shard_map/jit(dynamic_index_in_dim)/dynamic_slice | solution.py:296
  280.5 8.3 %pad_maximum_fusion = bf16[2,3072,768]{2,1,0:T(8,128)(2,1)} fusion(bf16[1,3072,768]{2,1,0:T(8,128)(2,1)} %get-tuple-element.30, bf16[1,3072,768]{2,1,0:T(8,128)(2,1)} %get-tuple-element.31), kind=kLoop, calls=%fused_computation.1 | loop fusion | flops 4718592 | bytes 18874368 | tf_op jit(solution)/shard_map/stack | solution.py:298
  289.3 14.6 %collective-permute-done.23 = bf16[2,3072,768]{2,1,0:T(8,128)(2,1)} collective-permute-done((bf16[2,3072,768]{2,1,0:T(8,128)(2,1)}, bf16[2,3072,768]{2,1,0:T(8,128)(2,1)}, u32[]{:S(2)}, u32[]{:S(2)}) %collective-permute-start.23) | collective-permute-done | bytes 9437216 | tf_op jit(solution)/shard_map/ppermute | solution.py:252
  303.9 7.3 %convert_add_fusion = f32[2,3072,768]{2,1,0:T(8,128)S(1)} fusion(bf16[2,3072,768]{2,1,0:T(8,128)(2,1)} %collective-permute-done.23, bf16[1,3072,768]{2,1,0:T(8,128)(2,1)} %get-tuple-element.32, bf16[1,3072,768]{2,1,0:T(8,128)(2,1)} %get-tuple-element.29), kind=kLoop, calls=%fused_computation | loop fusion | flops 18874368 | bytes 37748736 | tf_op jit(solution)/shard_map/add | solution.py:299
  311.2 7.2 %fusion.101 = (f32[1,3072,768]{2,1,0:T(8,128)}, f32[1,3072,768]{2,1,0:T(8,128)}) fusion(f32[2,3072,768]{2,1,0:T(8,128)S(1)} %convert_add_fusion), kind=kLoop, calls=%fused_computation.335 | loop fusion | bytes 37748736 | tf_op jit(solution)/shard_map/slice | solution.py:302
  318.4 3.7 dynamic-slice_bitcast_fusion.1
  334.3 20.4 %collective-permute-done.32 = bf16[2,4,192,384]{3,2,1,0:T(8,128)(2,1)S(1)} collective-permute-done((bf16[2,4,192,384]{3,2,1,0:T(8,128)(2,1)S(1)}, bf16[2,4,192,384]{3,2,1,0:T(8,128)(2,1)S(1)}, u32[]{:S(2)}, u32[]{:S(2)}) %collective-permute-start.32) | collective-permute-done | bytes 1179680 | tf_op jit(solution)/shard_map/ppermute | solution.py:176
  356.7 6.4 %add_convert_fusion.2 = bf16[512,768]{1,0:T(8,128)(2,1)} fusion(f32[512,768]{1,0:T(8,128)S(1)} %copy-done.4, bf16[512,3072]{1,0:T(8,128)(2,1)} %get-tuple-element.33, bf16[1536,768]{1,0:T(8,128)(2,1)S(1)} %copy-done.31, bf16[1536,768]{1,0:T(8,128)(2,1)S(1)} %copy-done.29, pred[]{:T(512)S(6)} %eq.60), kind=kOutput, calls=%fused_computation.73 | convolution fusion | flops 2437939200 | bytes 10223617 | tf_op jit(solution)/shard_map/dot_general | solution.py:35
  366.0 7.1 %collective-permute-done.35 = bf16[4,192,384]{2,1,0:T(8,128)(2,1)S(1)} collective-permute-done((bf16[4,192,384]{2,1,0:T(8,128)(2,1)}, bf16[4,192,384]{2,1,0:T(8,128)(2,1)S(1)}, u32[]{:S(2)}, u32[]{:S(2)}) %collective-permute-start.35) | collective-permute-done | bytes 589856 | tf_op jit(solution)/shard_map/ppermute | solution.py:176
  383.1 3.8 collective-permute-start.29
  390.5 6.0 %collective-permute-start.37 = (bf16[1,192,768]{2,1,0:T(8,128)(2,1)S(1)}, bf16[1,192,768]{2,1,0:T(8,128)(2,1)S(1)}, u32[]{:S(2)}, u32[]{:S(2)}) collective-permute-start(bf16[1,192,768]{2,1,0:T(8,128)(2,1)S(1)} %get-tuple-element.70), channel_id=1, source_target_pairs={{0,64},{32,96},{64,0},{96,32},{1,65},{33,97},{65,1},{97,33},{2,66}... | collective-permute-start | bytes 884744 | tf_op jit(solution)/shard_map/ppermute | solution.py:176
  410.6 6.7 %collective-permute-done.40 = bf16[192,768]{1,0:T(8,128)(2,1)S(1)} collective-permute-done((bf16[192,768]{1,0:T(8,128)(2,1)S(1)}, bf16[192,768]{1,0:T(8,128)(2,1)S(1)}, u32[]{:S(2)}, u32[]{:S(2)}) %collective-permute-start.40) | collective-permute-done | bytes 294944 | tf_op jit(solution)/shard_map/ppermute | solution.py:312
  425.1 7.5 %collective-permute-done.41 = bf16[192,768]{1,0:T(8,128)(2,1)S(1)} collective-permute-done((bf16[192,768]{1,0:T(8,128)(2,1)S(1)}, bf16[192,768]{1,0:T(8,128)(2,1)S(1)}, u32[]{:S(2)}, u32[]{:S(2)}) %collective-permute-start.41) | collective-permute-done | bytes 294944 | tf_op jit(solution)/shard_map/ppermute | solution.py:176
  441.8 7.4 %collective-permute-start.21 = (bf16[256,1536]{1,0:T(8,128)(2,1)}, bf16[256,1536]{1,0:T(8,128)(2,1)}, u32[]{:S(2)}, u32[]{:S(2)}) collective-permute-start(bf16[256,1536]{1,0:T(8,128)(2,1)} %get-tuple-element.91), channel_id=1, source_target_pairs={{0,0},{1,2},{2,1},{3,3},{4,4},{5,6},{6,5},{7,7},{8,8},{9,10},{10,9... | collective-permute-start | bytes 2359304 | tf_op jit(solution)/shard_map/ppermute | solution.py:339
  449.2 13.3 %collective-permute-done.45 = bf16[768,768]{1,0:T(8,128)(2,1)S(1)} collective-permute-done((bf16[768,768]{1,0:T(8,128)(2,1)S(1)}, bf16[768,768]{1,0:T(8,128)(2,1)S(1)}, u32[]{:S(2)}, u32[]{:S(2)}) %collective-permute-start.45) | collective-permute-done | bytes 1179680 | tf_op jit(solution)/shard_map/ppermute | solution.py:176
  (455 shorter events, 258.4 us)
Async XLA Ops:
  2.6 20.5 %collective-permute-start.2 = (bf16[144,768]{1,0:T(8,128)(2,1)}, bf16[144,768]{1,0:T(8,128)(2,1)}, u32[]{:S(2)}, u32[]{:S(2)}) collective-permute-start(bf16[144,768]{1,0:T(8,128)(2,1)} %fusion.68), channel_id=1, source_target_pairs={{0,6},{2,4},{4,2},{6,0},{1,7},{3,5},{5,3},{7,1},{8,14},{10,12},{12... | collective-permute-start | bytes 663560 | tf_op jit(solution)/shard_map/ppermute | solution.py:248
  7.4 28.9 %collective-permute-start.8 = (bf16[240,768]{1,0:T(8,128)(2,1)}, bf16[240,768]{1,0:T(8,128)(2,1)}, u32[]{:S(2)}, u32[]{:S(2)}) collective-permute-start(bf16[240,768]{1,0:T(8,128)(2,1)} %fusion.65), channel_id=1, source_target_pairs={{0,6},{2,4},{4,2},{6,0},{1,7},{3,5},{5,3},{7,1},{8,14},{10,12},{12... | collective-permute-start | bytes 1105928 | tf_op jit(solution)/shard_map/ppermute | solution.py:248
  8.9 45.2 %collective-permute-start.14 = (bf16[96,3072]{1,0:T(8,128)(2,1)}, bf16[96,3072]{1,0:T(8,128)(2,1)S(1)}, u32[]{:S(2)}, u32[]{:S(2)}) collective-permute-start(bf16[96,3072]{1,0:T(8,128)(2,1)} %fusion.39), channel_id=1, source_target_pairs={{0,6},{2,4},{4,2},{6,0},{1,7},{3,5},{5,3},{7,1},{8,14},{10,12},{12... | collective-permute-start | bytes 1769480 | tf_op jit(solution)/shard_map/ppermute | solution.py:248
  15.4 42.2 %collective-permute-start = (bf16[256,1536]{1,0:T(8,128)(2,1)}, bf16[256,1536]{1,0:T(8,128)(2,1)S(1)}, u32[]{:S(2)}, u32[]{:S(2)}) collective-permute-start(bf16[256,1536]{1,0:T(8,128)(2,1)} %get-tuple-element.93), channel_id=1, source_target_pairs={{0,0},{1,2},{2,1},{3,3},{4,4},{5,6},{6,5},{7,7},{8,8},{9,10},{10,9... | collective-permute-start | bytes 2359304 | tf_op jit(solution)/shard_map/ppermute | solution.py:328
  17.2 41.5 %collective-permute-start.1 = (bf16[256,1536]{1,0:T(8,128)(2,1)}, bf16[256,1536]{1,0:T(8,128)(2,1)S(1)}, u32[]{:S(2)}, u32[]{:S(2)}) collective-permute-start(bf16[256,1536]{1,0:T(8,128)(2,1)} %get-tuple-element.94), channel_id=1, source_target_pairs={{0,2},{1,0},{2,3},{3,1},{4,6},{5,4},{6,7},{7,5},{8,10},{9,8},{10,1... | collective-permute-start | bytes 2359304 | tf_op jit(solution)/shard_map/ppermute | solution.py:329
  23.1 17.4 %collective-permute-start.3 = (bf16[144,768]{1,0:T(8,128)(2,1)}, bf16[144,768]{1,0:T(8,128)(2,1)S(1)}, u32[]{:S(2)}, u32[]{:S(2)}) collective-permute-start(bf16[144,768]{1,0:T(8,128)(2,1)} %collective-permute-done.2), channel_id=1, source_target_pairs={{0,96},{32,0},{64,32},{96,64},{1,97},{33,1},{65,33},{97,65},{2,98}... | collective-permute-start | bytes 663560 | tf_op jit(solution)/shard_map/ppermute | solution.py:176
  54.0 28.8 %collective-permute-start.6 = (bf16[1152,768]{1,0:T(8,128)(2,1)S(1)}, bf16[1152,768]{1,0:T(8,128)(2,1)S(1)}, u32[]{:S(2)}, u32[]{:S(2)}) collective-permute-start(bf16[1152,768]{1,0:T(8,128)(2,1)S(1)} %pad_maximum_fusion.6), channel_id=1, source_target_pairs={{0,1},{1,0},{2,3},{3,2},{4,5},{5,4},{6,7},{7,6},{8,9},{9,8},{10,11... | collective-permute-start | bytes 5308424 | tf_op jit(solution)/shard_map/ppermute | solution.py:252
  54.1 17.0 %collective-permute-start.16 = (bf16[96,3072]{1,0:T(8,128)(2,1)S(1)}, bf16[96,3072]{1,0:T(8,128)(2,1)S(1)}, u32[]{:S(2)}, u32[]{:S(2)}) collective-permute-start(bf16[96,3072]{1,0:T(8,128)(2,1)S(1)} %collective-permute-done.14), channel_id=1, source_target_pairs={{0,32},{32,64},{64,96},{96,0},{1,33},{33,65},{65,97},{97,1},{2,34}... | collective-permute-start | bytes 1769480 | tf_op jit(solution)/shard_map/ppermute | solution.py:176
  57.3 15.8 %collective-permute-start.15 = (bf16[96,3072]{1,0:T(8,128)(2,1)S(1)}, bf16[96,3072]{1,0:T(8,128)(2,1)S(1)}, u32[]{:S(2)}, u32[]{:S(2)}) collective-permute-start(bf16[96,3072]{1,0:T(8,128)(2,1)S(1)} %collective-permute-done.14), channel_id=1, source_target_pairs={{0,96},{32,0},{64,32},{96,64},{1,97},{33,1},{65,33},{97,65},{2,98}... | collective-permute-start | bytes 1769480 | tf_op jit(solution)/shard_map/ppermute | solution.py:176
  71.0 68.9 %collective-permute-start.13 = (bf16[1920,768]{1,0:T(8,128)(2,1)}, bf16[1920,768]{1,0:T(8,128)(2,1)}, u32[]{:S(2)}, u32[]{:S(2)}) collective-permute-start(bf16[1920,768]{1,0:T(8,128)(2,1)} %pad_maximum_fusion.3), channel_id=1, source_target_pairs={{0,1},{1,0},{2,3},{3,2},{4,5},{5,4},{6,7},{7,6},{8,9},{9,8},{10,11... | collective-permute-start | bytes 8847368 | tf_op jit(solution)/shard_map/ppermute | solution.py:252
  96.0 16.5 %collective-permute-start.7 = (bf16[512,1536]{1,0:T(8,128)(2,1)}, bf16[512,1536]{1,0:T(8,128)(2,1)}, u32[]{:S(2)}, u32[]{:S(2)}) collective-permute-start(bf16[512,1536]{1,0:T(8,128)(2,1)} %pad_maximum_fusion.7), channel_id=1, source_target_pairs={{0,1},{1,0},{2,3},{3,2},{4,5},{5,4},{6,7},{7,6},{8,9},{9,8},{10,11... | collective-permute-start | bytes 4718600 | tf_op jit(solution)/shard_map/ppermute | solution.py:252
  99.7 55.3 %collective-permute-start.19 = (bf16[768,3072]{1,0:T(8,128)(2,1)}, bf16[768,3072]{1,0:T(8,128)(2,1)}, u32[]{:S(2)}, u32[]{:S(2)}) collective-permute-start(bf16[768,3072]{1,0:T(8,128)(2,1)} %pad_maximum_fusion.1), channel_id=1, source_target_pairs={{0,1},{1,0},{2,3},{3,2},{4,5},{5,4},{6,7},{7,6},{8,9},{9,8},{10,11... | collective-permute-start | bytes 14155784 | tf_op jit(solution)/shard_map/ppermute | solution.py:252
  236.5 20.9 %collective-permute-start.20 = (f32[512,1536]{1,0:T(8,128)S(1)}, f32[512,1536]{1,0:T(8,128)S(1)}, u32[]{:S(2)}, u32[]{:S(2)}) collective-permute-start(f32[512,1536]{1,0:T(8,128)S(1)} %slice.402), channel_id=1, source_target_pairs={{0,1},{1,0},{2,3},{3,2},{4,5},{5,4},{6,7},{7,6},{8,9},{9,8},{10,11... | collective-permute-start | bytes 9437192 | tf_op jit(solution)/shard_map/ppermute | solution.py:252
  324.6 30.1 %collective-permute-start.32 = (bf16[2,4,192,384]{3,2,1,0:T(8,128)(2,1)S(1)}, bf16[2,4,192,384]{3,2,1,0:T(8,128)(2,1)S(1)}, u32[]{:S(2)}, u32[]{:S(2)}) collective-permute-start(bf16[2,4,192,384]{3,2,1,0:T(8,128)(2,1)S(1)} %pad_maximum_fusion.10), channel_id=1, source_target_pairs={{0,8},{8,16},{16,24},{24,0},{1,9},{9,17},{17,25},{25,1},{2,10},{10... | collective-permute-start | bytes 3538952 | tf_op jit(solution)/shard_map/ppermute | solution.py:176
  328.4 34.7 %collective-permute-start.25 = (bf16[2,768,384]{2,1,0:T(8,128)(2,1)S(1)}, bf16[2,768,384]{2,1,0:T(8,128)(2,1)S(1)}, u32[]{:S(2)}, u32[]{:S(2)}) collective-permute-start(bf16[2,768,384]{2,1,0:T(8,128)(2,1)S(1)} %pad_maximum_fusion.9), channel_id=1, source_target_pairs={{0,96},{32,0},{64,32},{96,64},{1,97},{33,1},{65,33},{97,65},{2,98}... | collective-permute-start | bytes 3538952 | tf_op jit(solution)/shard_map/ppermute | solution.py:176
  331.2 34.5 %collective-permute-start.24 = (bf16[2,768,384]{2,1,0:T(8,128)(2,1)S(1)}, bf16[2,768,384]{2,1,0:T(8,128)(2,1)S(1)}, u32[]{:S(2)}, u32[]{:S(2)}) collective-permute-start(bf16[2,768,384]{2,1,0:T(8,128)(2,1)S(1)} %pad_maximum_fusion.8), channel_id=1, source_target_pairs={{0,32},{32,64},{64,96},{96,0},{1,33},{33,65},{65,97},{97,1},{2,34}... | collective-permute-start | bytes 3538952 | tf_op jit(solution)/shard_map/ppermute | solution.py:176
  331.6 34.4 %collective-permute-start.33 = (bf16[2,4,192,384]{3,2,1,0:T(8,128)(2,1)S(1)}, bf16[2,4,192,384]{3,2,1,0:T(8,128)(2,1)S(1)}, u32[]{:S(2)}, u32[]{:S(2)}) collective-permute-start(bf16[2,4,192,384]{3,2,1,0:T(8,128)(2,1)S(1)} %pad_maximum_fusion.11), channel_id=1, source_target_pairs={{0,24},{8,0},{16,8},{24,16},{1,25},{9,1},{17,9},{25,17},{2,26},{10... | collective-permute-start | bytes 3538952 | tf_op jit(solution)/shard_map/ppermute | solution.py:176
  356.7 16.5 %collective-permute-start.35 = (bf16[4,192,384]{2,1,0:T(8,128)(2,1)}, bf16[4,192,384]{2,1,0:T(8,128)(2,1)S(1)}, u32[]{:S(2)}, u32[]{:S(2)}) collective-permute-start(bf16[4,192,384]{2,1,0:T(8,128)(2,1)} %fusion.11), channel_id=1, source_target_pairs={{0,8},{8,16},{16,24},{24,0},{1,9},{9,17},{17,25},{25,1},{2,10},{10... | collective-permute-start | bytes 1769480 | tf_op jit(solution)/shard_map/ppermute | solution.py:176
  365.9 16.0 %collective-permute-start.27 = (bf16[768,384]{1,0:T(8,128)(2,1)S(1)}, bf16[768,384]{1,0:T(8,128)(2,1)S(1)}, u32[]{:S(2)}, u32[]{:S(2)}) collective-permute-start(bf16[768,384]{1,0:T(8,128)(2,1)S(1)} %fusion.15), channel_id=1, source_target_pairs={{0,32},{32,64},{64,96},{96,0},{1,33},{33,65},{65,97},{97,1},{2,34}... | collective-permute-start | bytes 1769480 | tf_op jit(solution)/shard_map/ppermute | solution.py:176
  373.5 16.3 %collective-permute-start.34 = (bf16[4,192,384]{2,1,0:T(8,128)(2,1)S(1)}, bf16[4,192,384]{2,1,0:T(8,128)(2,1)S(1)}, u32[]{:S(2)}, u32[]{:S(2)}) collective-permute-start(bf16[4,192,384]{2,1,0:T(8,128)(2,1)S(1)} %get-tuple-element.37), channel_id=1, source_target_pairs={{0,24},{8,0},{16,8},{24,16},{1,25},{9,1},{17,9},{25,17},{2,26},{10... | collective-permute-start | bytes 1769480 | tf_op jit(solution)/shard_map/ppermute | solution.py:176
  436.4 26.0 %collective-permute-start.45 = (bf16[768,768]{1,0:T(8,128)(2,1)S(1)}, bf16[768,768]{1,0:T(8,128)(2,1)S(1)}, u32[]{:S(2)}, u32[]{:S(2)}) collective-permute-start(bf16[768,768]{1,0:T(8,128)(2,1)S(1)} %get-tuple-element.20), channel_id=1, source_target_pairs={{0,32},{32,64},{64,96},{96,0},{1,33},{33,65},{65,97},{97,1},{2,34}... | collective-permute-start | bytes 3538952 | tf_op jit(solution)/shard_map/ppermute | solution.py:176
  436.7 25.9 %collective-permute-start.44 = (bf16[768,768]{1,0:T(8,128)(2,1)S(1)}, bf16[768,768]{1,0:T(8,128)(2,1)S(1)}, u32[]{:S(2)}, u32[]{:S(2)}) collective-permute-start(bf16[768,768]{1,0:T(8,128)(2,1)S(1)} %get-tuple-element.20), channel_id=1, source_target_pairs={{0,96},{32,0},{64,32},{96,64},{1,97},{33,1},{65,33},{97,65},{2,98}... | collective-permute-start | bytes 3538952 | tf_op jit(solution)/shard_map/ppermute | solution.py:176
  441.8 24.2 %collective-permute-start.21 = (bf16[256,1536]{1,0:T(8,128)(2,1)}, bf16[256,1536]{1,0:T(8,128)(2,1)}, u32[]{:S(2)}, u32[]{:S(2)}) collective-permute-start(bf16[256,1536]{1,0:T(8,128)(2,1)} %get-tuple-element.91), channel_id=1, source_target_pairs={{0,0},{1,2},{2,1},{3,3},{4,4},{5,6},{6,5},{7,7},{8,8},{9,10},{10,9... | collective-permute-start | bytes 2359304 | tf_op jit(solution)/shard_map/ppermute | solution.py:339
  449.2 16.7 %collective-permute-start.22 = (bf16[256,1536]{1,0:T(8,128)(2,1)}, bf16[256,1536]{1,0:T(8,128)(2,1)}, u32[]{:S(2)}, u32[]{:S(2)}) collective-permute-start(bf16[256,1536]{1,0:T(8,128)(2,1)} %get-tuple-element.92), channel_id=1, source_target_pairs={{2,0},{0,1},{3,2},{1,3},{6,4},{4,5},{7,6},{5,7},{10,8},{8,9},{11,1... | collective-permute-start | bytes 2359304 | tf_op jit(solution)/shard_map/ppermute | solution.py:340
  (115 other events, 1052.8 us)

commit v3 on v1

--- a/solution.py
+++ b/solution.py
@@ -70,7 +70,7 @@
         highest = jnp.max(scores, axis=1, keepdims=True)
         expd = jnp.exp(scores - highest)
         total = jnp.sum(expd, axis=1, keepdims=True)
-        probs_low = (expd / total).astype(jnp.bfloat16)
+        probs_low = (expd * (1.0 / total)).astype(jnp.bfloat16)
         o_ref[:, cols] = jnp.dot(probs_low, v_ref[:, cols], preferred_element_type=jnp.float32)
         lse_ref[:, h:h + 1] = highest + jnp.log(total)
 

time: 481 us -> 481 us (level)
  no operation moved by 1% of the time
where the time goes in v3:
time: 481 us; the launch traced here: 472 us
  waiting for transfers between devices  120 us (25%)
  local copies, waits for them, and re-layouts  77.7 us (16%)
  starting transfers between devices  75.6 us (16%)
  matrix products  72.3 us (15%)
  other arithmetic  69.2 us (14%)
  Pallas kernels  54.7 us (11%)
    ppermute x32, waiting for transfers between devices, shift(): return lax.ppermute(x, axis, [(i, (i + step) % n) for i in range(n)])  79.1 us
    ppermute x32, starting transfers between devices, shift(): return lax.ppermute(x, axis, [(i, (i + step) % n) for i in range(n)])  53.4 us
    pallas_call x1, Pallas kernels, attention_backward(): pl.pallas_call(attention_backward_kernel, grid=(pairs,), in_specs=[pl.Blo...  31 us
    dot_general x7, matrix products, matmul(): return jnp.dot(left, right, preferred_element_type=jnp.float32)  30.1 us
    dot_general x13, matrix products, contract_rows(): lax.dot_general(left, right, (((0,), (0,)), ((), ())), preferred_element_...  24.2 us
    pallas_call x1, Pallas kernels, attention_forward(): pl.pallas_call(attention_forward_kernel, grid=(pairs,), in_specs=[pl.Bloc...  23.6 us
    dot_general x7, matrix products, contract_cols(): lax.dot_general(left, right, (((1,), (1,)), ((), ())), preferred_element_...  18.1 us
    ppermute x1, waiting for transfers between devices, from_sequence(): second = lax.ppermute(second, GRP, [(2, 0), (0, 1), (3, 2), (1, 3)])  15.6 us
  transfers between devices with their start and end apart: 48, of which 19 were waited for; matrix products, arithmetic and copies ran while one was open for 22% of the time, Pallas kernels for 5%

profile of v3, /device:TPU:0, one launch (start us, length us, event | category | flops | bytes accessed | tf_op | source)
XLA Modules:
  0.0 472.3 jit_solution(16833785302817547647)
XLA Ops:
  28.3 9.0 %collective-permute-done.8 = bf16[240,768]{1,0:T(8,128)(2,1)} collective-permute-done((bf16[240,768]{1,0:T(8,128)(2,1)}, bf16[240,768]{1,0:T(8,128)(2,1)}, u32[]{:S(2)}, u32[]{:S(2)}) %collective-permute-start.8) | collective-permute-done | bytes 368672 | tf_op jit(solution)/shard_map/ppermute | solution.py:248
  103.3 23.6 %shard_map.178 = (f32[512,768]{1,0:T(8,128)}, f32[6,512,2]{2,1,0:T(8,128)}) custom-call(bf16[512,768]{1,0:T(8,128)(2,1)} %copy.27.q_ref, bf16[1024,1536]{1,0:T(8,128)(2,1)} %pad_maximum_fusion.2.k_ref.v_ref, bf16[1024,1536]{1,0:T(8,128)(2,1)} %pad_maximum_fusion.2.k_ref.v_ref, s32[512,1]{1,0:T(8,128)} %iota_add_fusion.rq_ref, s32[512,1]{1,0:T(8,128)} %copy.28.sq_ref, ...), custom_call_target="tpu_custom_call" | custom-call | flops 1610612736 | bytes 5505024 | tf_op jit(solution)/shard_map/pallas_call | solution.py:118
  134.0 8.0 %fusion.20 = f32[512,3072]{1,0:T(8,128)} fusion(bf16[1536,768]{1,0:T(8,128)(2,1)S(1)} %get-tuple-element.119, bf16[1536,768]{1,0:T(8,128)(2,1)S(1)} %get-tuple-element.118, pred[]{:T(512)S(6)} %eq.70, bf16[512,1536]{1,0:T(8,128)(2,1)S(1)} %maximum_select_fusion.7), kind=kOutput, calls=%fused_computation.131 | convolution fusion | flops 2437152768 | bytes 11796481 | tf_op jit(solution)/shard_map/dot_general | solution.py:45
  151.7 4.7 fusion.23
  156.4 12.4 %multiply_convert_fusion.1 = (bf16[512,3072]{1,0:T(8,128)(2,1)}, bf16[512,3072]{1,0:T(8,128)(2,1)}, bf16[512,3072]{1,0:T(8,128)(2,1)}) fusion(f32[512,3072]{1,0:T(8,128)} %fusion.23, f32[512,3072]{1,0:T(8,128)} %fusion.20, bf16[512,768]{1,0:T(8,128)(2,1)S(1)} %multiply_convert_fusion.2, bf16[384,3072]{1,0:T(8,128)(2,1)S(1)} %copy-done.31, ...), kind=kOutput, calls=%fused_computation.5 | convolution fusion | flops 2465464320 | bytes 27525120 | tf_op jit(solution)/shard_map/dot_general | solution.py:35
  186.1 31.0 %shard_map.179 = (f32[512,768]{1,0:T(8,128)}, f32[1024,768]{1,0:T(8,128)}, f32[1024,768]{1,0:T(8,128)}) custom-call(bf16[512,768]{1,0:T(8,128)(2,1)} %copy.27.q_ref, bf16[1024,1536]{1,0:T(8,128)(2,1)} %pad_maximum_fusion.2.k_ref.v_ref, bf16[1024,1536]{1,0:T(8,128)(2,1)} %pad_maximum_fusion.2.k_ref.v_ref, bf16[512,768]{1,0:T(8,128)(2,1)} %convolution_convert_fusion.13.do_ref, ...), custom_call_target="tpu_custom_call" | custom-call | flops 4026531840 | bytes 12582912 | tf_op jit(solution)/shard_map/pallas_call | solution.py:147
  239.8 4.5 convolution_convert_fusion
  260.8 6.5 %constant_dynamic-slice_fusion.3 = (bf16[1,3072,768]{2,1,0:T(8,128)(2,1)}, bf16[1,3072,768]{2,1,0:T(8,128)(2,1)}, bf16[1,3072,768]{2,1,0:T(8,128)(2,1)}, bf16[1,3072,768]{2,1,0:T(8,128)(2,1)}) fusion(bf16[4,3072,768]{2,1,0:T(8,128)(2,1)S(1)} %constant_dynamic-update-slice_fusion.4, s32[]{:T(128)S(6)} %select_n.453, s32[]{:T(128)S(6)} %select_n.456, ...), kind=kLoop, calls=%fused_computation.251 | loop fusion | bytes 37748752 | tf_op jit(solution)/shard_map/jit(dynamic_index_in_dim)/dynamic_slice | solution.py:296
  267.4 8.4 %pad_maximum_fusion = bf16[2,3072,768]{2,1,0:T(8,128)(2,1)} fusion(bf16[1,3072,768]{2,1,0:T(8,128)(2,1)} %get-tuple-element.28, bf16[1,3072,768]{2,1,0:T(8,128)(2,1)} %get-tuple-element.29), kind=kLoop, calls=%fused_computation.1 | loop fusion | flops 4718592 | bytes 18874368 | tf_op jit(solution)/shard_map/stack | solution.py:298
  276.0 8.2 %add_convert_fusion.2 = bf16[512,768]{1,0:T(8,128)(2,1)} fusion(f32[512,768]{1,0:T(8,128)S(1)} %copy-done.5, bf16[512,3072]{1,0:T(8,128)(2,1)} %get-tuple-element.31, bf16[1536,768]{1,0:T(8,128)(2,1)} %copy-done.27, bf16[1536,768]{1,0:T(8,128)(2,1)} %copy-done.26, pred[]{:T(512)S(6)} %eq.70), kind=kOutput, calls=%fused_computation.73 | convolution fusion | flops 2437939200 | bytes 10223617 | tf_op jit(solution)/shard_map/dot_general | solution.py:35
  284.2 6.6 %collective-permute-done.23 = bf16[2,3072,768]{2,1,0:T(8,128)(2,1)} collective-permute-done((bf16[2,3072,768]{2,1,0:T(8,128)(2,1)}, bf16[2,3072,768]{2,1,0:T(8,128)(2,1)}, u32[]{:S(2)}, u32[]{:S(2)}) %collective-permute-start.23) | collective-permute-done | bytes 9437216 | tf_op jit(solution)/shard_map/ppermute | solution.py:252
  290.8 7.5 %convert_add_fusion = f32[2,3072,768]{2,1,0:T(8,128)S(1)} fusion(bf16[2,3072,768]{2,1,0:T(8,128)(2,1)} %collective-permute-done.23, bf16[1,3072,768]{2,1,0:T(8,128)(2,1)} %get-tuple-element.30, bf16[1,3072,768]{2,1,0:T(8,128)(2,1)} %get-tuple-element.27), kind=kLoop, calls=%fused_computation | loop fusion | flops 18874368 | bytes 37748736 | tf_op jit(solution)/shard_map/add | solution.py:299
  298.2 7.0 %fusion.101 = (f32[1,3072,768]{2,1,0:T(8,128)}, f32[1,3072,768]{2,1,0:T(8,128)}) fusion(f32[2,3072,768]{2,1,0:T(8,128)S(1)} %convert_add_fusion), kind=kLoop, calls=%fused_computation.296 | loop fusion | bytes 37748736 | tf_op jit(solution)/shard_map/slice | solution.py:302
  321.5 21.2 %collective-permute-done.32 = bf16[2,4,192,384]{3,2,1,0:T(8,128)(2,1)S(1)} collective-permute-done((bf16[2,4,192,384]{3,2,1,0:T(8,128)(2,1)S(1)}, bf16[2,4,192,384]{3,2,1,0:T(8,128)(2,1)S(1)}, u32[]{:S(2)}, u32[]{:S(2)}) %collective-permute-start.32) | collective-permute-done | bytes 1179680 | tf_op jit(solution)/shard_map/ppermute | solution.py:176
  347.4 11.4 %collective-permute-done.35 = bf16[4,192,384]{2,1,0:T(8,128)(2,1)S(1)} collective-permute-done((bf16[4,192,384]{2,1,0:T(8,128)(2,1)S(1)}, bf16[4,192,384]{2,1,0:T(8,128)(2,1)S(1)}, u32[]{:S(2)}, u32[]{:S(2)}) %collective-permute-start.35) | collective-permute-done | bytes 589856 | tf_op jit(solution)/shard_map/ppermute | solution.py:176
  363.3 4.4 collective-permute-start.29
  367.7 9.6 %collective-permute-done.34 = bf16[4,192,384]{2,1,0:T(8,128)(2,1)S(1)} collective-permute-done((bf16[4,192,384]{2,1,0:T(8,128)(2,1)S(1)}, bf16[4,192,384]{2,1,0:T(8,128)(2,1)S(1)}, u32[]{:S(2)}, u32[]{:S(2)}) %collective-permute-start.34) | collective-permute-done | bytes 589856 | tf_op jit(solution)/shard_map/ppermute | solution.py:176
  377.7 4.5 collective-permute-start.37
  395.5 5.4 %collective-permute-done.40 = bf16[192,768]{1,0:T(8,128)(2,1)S(1)} collective-permute-done((bf16[192,768]{1,0:T(8,128)(2,1)S(1)}, bf16[192,768]{1,0:T(8,128)(2,1)S(1)}, u32[]{:S(2)}, u32[]{:S(2)}) %collective-permute-start.40) | collective-permute-done | bytes 294944 | tf_op jit(solution)/shard_map/ppermute | solution.py:312
  408.9 6.6 %collective-permute-done.41 = bf16[192,768]{1,0:T(8,128)(2,1)S(1)} collective-permute-done((bf16[192,768]{1,0:T(8,128)(2,1)S(1)}, bf16[192,768]{1,0:T(8,128)(2,1)S(1)}, u32[]{:S(2)}, u32[]{:S(2)}) %collective-permute-start.41) | collective-permute-done | bytes 294944 | tf_op jit(solution)/shard_map/ppermute | solution.py:176
  415.6 5.6 %collective-permute-start.45 = (bf16[768,768]{1,0:T(8,128)(2,1)S(1)}, bf16[768,768]{1,0:T(8,128)(2,1)S(1)}, u32[]{:S(2)}, u32[]{:S(2)}) collective-permute-start(bf16[768,768]{1,0:T(8,128)(2,1)S(1)} %constant_dynamic-update-slice_fusion.14), channel_id=1, source_target_pairs={{0,96},{32,0},{64,32},{96,64},{1,97},{33,1},{65,33},{97,65},{2,98}... | collective-permute-start | bytes 3538952 | tf_op jit(solution)/shard_map/ppermute | solution.py:176
  422.6 7.4 %collective-permute-start.21 = (bf16[256,1536]{1,0:T(8,128)(2,1)}, bf16[256,1536]{1,0:T(8,128)(2,1)}, u32[]{:S(2)}, u32[]{:S(2)}) collective-permute-start(bf16[256,1536]{1,0:T(8,128)(2,1)} %get-tuple-element.86), channel_id=1, source_target_pairs={{0,0},{1,2},{2,1},{3,3},{4,4},{5,6},{6,5},{7,7},{8,8},{9,10},{10,9... | collective-permute-start | bytes 2359304 | tf_op jit(solution)/shard_map/ppermute | solution.py:339
  430.0 15.6 %collective-permute-done.22 = bf16[256,1536]{1,0:T(8,128)(2,1)} collective-permute-done((bf16[256,1536]{1,0:T(8,128)(2,1)}, bf16[256,1536]{1,0:T(8,128)(2,1)}, u32[]{:S(2)}, u32[]{:S(2)}) %collective-permute-start.22) | collective-permute-done | bytes 786464 | tf_op jit(solution)/shard_map/ppermute | solution.py:340
  452.8 8.6 %collective-permute-done.47 = bf16[384,768]{1,0:T(8,128)(2,1)S(1)} collective-permute-done((bf16[384,768]{1,0:T(8,128)(2,1)S(1)}, bf16[384,768]{1,0:T(8,128)(2,1)S(1)}, u32[]{:S(2)}, u32[]{:S(2)}) %collective-permute-start.47) | collective-permute-done | bytes 589856 | tf_op jit(solution)/shard_map/ppermute | solution.py:176
  (415 shorter events, 232.0 us)
Async XLA Ops:
  2.6 23.0 %collective-permute-start.2 = (bf16[144,768]{1,0:T(8,128)(2,1)}, bf16[144,768]{1,0:T(8,128)(2,1)}, u32[]{:S(2)}, u32[]{:S(2)}) collective-permute-start(bf16[144,768]{1,0:T(8,128)(2,1)} %fusion.68), channel_id=1, source_target_pairs={{0,6},{2,4},{4,2},{6,0},{1,7},{3,5},{5,3},{7,1},{8,14},{10,12},{12... | collective-permute-start | bytes 663560 | tf_op jit(solution)/shard_map/ppermute | solution.py:248
  7.4 29.9 %collective-permute-start.8 = (bf16[240,768]{1,0:T(8,128)(2,1)}, bf16[240,768]{1,0:T(8,128)(2,1)}, u32[]{:S(2)}, u32[]{:S(2)}) collective-permute-start(bf16[240,768]{1,0:T(8,128)(2,1)} %fusion.65), channel_id=1, source_target_pairs={{0,6},{2,4},{4,2},{6,0},{1,7},{3,5},{5,3},{7,1},{8,14},{10,12},{12... | collective-permute-start | bytes 1105928 | tf_op jit(solution)/shard_map/ppermute | solution.py:248
  8.9 41.1 %collective-permute-start.14 = (bf16[96,3072]{1,0:T(8,128)(2,1)}, bf16[96,3072]{1,0:T(8,128)(2,1)}, u32[]{:S(2)}, u32[]{:S(2)}) collective-permute-start(bf16[96,3072]{1,0:T(8,128)(2,1)} %fusion.39), channel_id=1, source_target_pairs={{0,6},{2,4},{4,2},{6,0},{1,7},{3,5},{5,3},{7,1},{8,14},{10,12},{12... | collective-permute-start | bytes 1769480 | tf_op jit(solution)/shard_map/ppermute | solution.py:248
  14.0 45.7 %collective-permute-start = (bf16[256,1536]{1,0:T(8,128)(2,1)}, bf16[256,1536]{1,0:T(8,128)(2,1)S(1)}, u32[]{:S(2)}, u32[]{:S(2)}) collective-permute-start(bf16[256,1536]{1,0:T(8,128)(2,1)} %get-tuple-element.88), channel_id=1, source_target_pairs={{0,0},{1,2},{2,1},{3,3},{4,4},{5,6},{6,5},{7,7},{8,8},{9,10},{10,9... | collective-permute-start | bytes 2359304 | tf_op jit(solution)/shard_map/ppermute | solution.py:328
  15.8 45.5 %collective-permute-start.1 = (bf16[256,1536]{1,0:T(8,128)(2,1)S(1)}, bf16[256,1536]{1,0:T(8,128)(2,1)S(1)}, u32[]{:S(2)}, u32[]{:S(2)}) collective-permute-start(bf16[256,1536]{1,0:T(8,128)(2,1)S(1)} %get-tuple-element.89), channel_id=1, source_target_pairs={{0,2},{1,0},{2,3},{3,1},{4,6},{5,4},{6,7},{7,5},{8,10},{9,8},{10,1... | collective-permute-start | bytes 2359304 | tf_op jit(solution)/shard_map/ppermute | solution.py:329
  25.7 16.0 %collective-permute-start.3 = (bf16[144,768]{1,0:T(8,128)(2,1)}, bf16[144,768]{1,0:T(8,128)(2,1)S(1)}, u32[]{:S(2)}, u32[]{:S(2)}) collective-permute-start(bf16[144,768]{1,0:T(8,128)(2,1)} %collective-permute-done.2), channel_id=1, source_target_pairs={{0,32},{32,64},{64,96},{96,0},{1,33},{33,65},{65,97},{97,1},{2,34}... | collective-permute-start | bytes 663560 | tf_op jit(solution)/shard_map/ppermute | solution.py:176
  50.0 27.9 %collective-permute-start.6 = (bf16[1152,768]{1,0:T(8,128)(2,1)S(1)}, bf16[1152,768]{1,0:T(8,128)(2,1)S(1)}, u32[]{:S(2)}, u32[]{:S(2)}) collective-permute-start(bf16[1152,768]{1,0:T(8,128)(2,1)S(1)} %pad_maximum_fusion.6), channel_id=1, source_target_pairs={{0,1},{1,0},{2,3},{3,2},{4,5},{5,4},{6,7},{7,6},{8,9},{9,8},{10,11... | collective-permute-start | bytes 5308424 | tf_op jit(solution)/shard_map/ppermute | solution.py:252
  54.3 18.3 %collective-permute-start.16 = (bf16[96,3072]{1,0:T(8,128)(2,1)}, bf16[96,3072]{1,0:T(8,128)(2,1)S(1)}, u32[]{:S(2)}, u32[]{:S(2)}) collective-permute-start(bf16[96,3072]{1,0:T(8,128)(2,1)} %collective-permute-done.14), channel_id=1, source_target_pairs={{0,96},{32,0},{64,32},{96,64},{1,97},{33,1},{65,33},{97,65},{2,98}... | collective-permute-start | bytes 1769480 | tf_op jit(solution)/shard_map/ppermute | solution.py:176
  58.0 18.6 %collective-permute-start.15 = (bf16[96,3072]{1,0:T(8,128)(2,1)}, bf16[96,3072]{1,0:T(8,128)(2,1)S(1)}, u32[]{:S(2)}, u32[]{:S(2)}) collective-permute-start(bf16[96,3072]{1,0:T(8,128)(2,1)} %collective-permute-done.14), channel_id=1, source_target_pairs={{0,32},{32,64},{64,96},{96,0},{1,33},{33,65},{65,97},{97,1},{2,34}... | collective-permute-start | bytes 1769480 | tf_op jit(solution)/shard_map/ppermute | solution.py:176
  72.6 54.3 %collective-permute-start.13 = (bf16[1920,768]{1,0:T(8,128)(2,1)}, bf16[1920,768]{1,0:T(8,128)(2,1)}, u32[]{:S(2)}, u32[]{:S(2)}) collective-permute-start(bf16[1920,768]{1,0:T(8,128)(2,1)} %pad_maximum_fusion.3), channel_id=1, source_target_pairs={{0,1},{1,0},{2,3},{3,2},{4,5},{5,4},{6,7},{7,6},{8,9},{9,8},{10,11... | collective-permute-start | bytes 8847368 | tf_op jit(solution)/shard_map/ppermute | solution.py:252
  73.4 17.8 %collective-permute-start.18 = (bf16[48,3072]{1,0:T(8,128)(2,1)}, bf16[48,3072]{1,0:T(8,128)(2,1)}, u32[]{:S(2)}, u32[]{:S(2)}) collective-permute-start(bf16[48,3072]{1,0:T(8,128)(2,1)} %slice.395), channel_id=1, source_target_pairs={{0,96},{32,0},{64,32},{96,64},{1,97},{33,1},{65,33},{97,65},{2,98}... | collective-permute-start | bytes 884744 | tf_op jit(solution)/shard_map/ppermute | solution.py:176
  94.7 47.3 %collective-permute-start.19 = (bf16[768,3072]{1,0:T(8,128)(2,1)}, bf16[768,3072]{1,0:T(8,128)(2,1)}, u32[]{:S(2)}, u32[]{:S(2)}) collective-permute-start(bf16[768,3072]{1,0:T(8,128)(2,1)} %pad_maximum_fusion.1), channel_id=1, source_target_pairs={{0,1},{1,0},{2,3},{3,2},{4,5},{5,4},{6,7},{7,6},{8,9},{9,8},{10,11... | collective-permute-start | bytes 14155784 | tf_op jit(solution)/shard_map/ppermute | solution.py:252
  223.7 20.6 %collective-permute-start.20 = (f32[512,1536]{1,0:T(8,128)S(1)}, f32[512,1536]{1,0:T(8,128)S(1)}, u32[]{:S(2)}, u32[]{:S(2)}) collective-permute-start(f32[512,1536]{1,0:T(8,128)S(1)} %slice.409), channel_id=1, source_target_pairs={{0,1},{1,0},{2,3},{3,2},{4,5},{5,4},{6,7},{7,6},{8,9},{9,8},{10,11... | collective-permute-start | bytes 9437192 | tf_op jit(solution)/shard_map/ppermute | solution.py:252
  313.3 29.4 %collective-permute-start.32 = (bf16[2,4,192,384]{3,2,1,0:T(8,128)(2,1)S(1)}, bf16[2,4,192,384]{3,2,1,0:T(8,128)(2,1)S(1)}, u32[]{:S(2)}, u32[]{:S(2)}) collective-permute-start(bf16[2,4,192,384]{3,2,1,0:T(8,128)(2,1)S(1)} %pad_maximum_fusion.10), channel_id=1, source_target_pairs={{0,8},{8,16},{16,24},{24,0},{1,9},{9,17},{17,25},{25,1},{2,10},{10... | collective-permute-start | bytes 3538952 | tf_op jit(solution)/shard_map/ppermute | solution.py:176
  313.5 30.3 %collective-permute-start.25 = (bf16[2,768,384]{2,1,0:T(8,128)(2,1)S(1)}, bf16[2,768,384]{2,1,0:T(8,128)(2,1)S(1)}, u32[]{:S(2)}, u32[]{:S(2)}) collective-permute-start(bf16[2,768,384]{2,1,0:T(8,128)(2,1)S(1)} %pad_maximum_fusion.9), channel_id=1, source_target_pairs={{0,96},{32,0},{64,32},{96,64},{1,97},{33,1},{65,33},{97,65},{2,98}... | collective-permute-start | bytes 3538952 | tf_op jit(solution)/shard_map/ppermute | solution.py:176
  317.1 30.0 %collective-permute-start.24 = (bf16[2,768,384]{2,1,0:T(8,128)(2,1)S(1)}, bf16[2,768,384]{2,1,0:T(8,128)(2,1)S(1)}, u32[]{:S(2)}, u32[]{:S(2)}) collective-permute-start(bf16[2,768,384]{2,1,0:T(8,128)(2,1)S(1)} %pad_maximum_fusion.8), channel_id=1, source_target_pairs={{0,32},{32,64},{64,96},{96,0},{1,33},{33,65},{65,97},{97,1},{2,34}... | collective-permute-start | bytes 3538952 | tf_op jit(solution)/shard_map/ppermute | solution.py:176
  317.4 30.0 %collective-permute-start.33 = (bf16[2,4,192,384]{3,2,1,0:T(8,128)(2,1)S(1)}, bf16[2,4,192,384]{3,2,1,0:T(8,128)(2,1)S(1)}, u32[]{:S(2)}, u32[]{:S(2)}) collective-permute-start(bf16[2,4,192,384]{3,2,1,0:T(8,128)(2,1)S(1)} %pad_maximum_fusion.11), channel_id=1, source_target_pairs={{0,24},{8,0},{16,8},{24,16},{1,25},{9,1},{17,9},{25,17},{2,26},{10... | collective-permute-start | bytes 3538952 | tf_op jit(solution)/shard_map/ppermute | solution.py:176
  343.9 16.4 %collective-permute-start.26 = (bf16[768,384]{1,0:T(8,128)(2,1)S(1)}, bf16[768,384]{1,0:T(8,128)(2,1)S(1)}, u32[]{:S(2)}, u32[]{:S(2)}) collective-permute-start(bf16[768,384]{1,0:T(8,128)(2,1)S(1)} %fusion.17), channel_id=1, source_target_pairs={{0,96},{32,0},{64,32},{96,64},{1,97},{33,1},{65,33},{97,65},{2,98}... | collective-permute-start | bytes 1769480 | tf_op jit(solution)/shard_map/ppermute | solution.py:176
  359.1 18.2 %collective-permute-start.34 = (bf16[4,192,384]{2,1,0:T(8,128)(2,1)S(1)}, bf16[4,192,384]{2,1,0:T(8,128)(2,1)S(1)}, u32[]{:S(2)}, u32[]{:S(2)}) collective-permute-start(bf16[4,192,384]{2,1,0:T(8,128)(2,1)S(1)} %get-tuple-element.35), channel_id=1, source_target_pairs={{0,24},{8,0},{16,8},{24,16},{1,25},{9,1},{17,9},{25,17},{2,26},{10... | collective-permute-start | bytes 1769480 | tf_op jit(solution)/shard_map/ppermute | solution.py:176
  363.3 18.9 %collective-permute-start.28 = (bf16[192,768]{1,0:T(8,128)(2,1)S(1)}, bf16[192,768]{1,0:T(8,128)(2,1)S(1)}, u32[]{:S(2)}, u32[]{:S(2)}) collective-permute-start(bf16[192,768]{1,0:T(8,128)(2,1)S(1)} %get-tuple-element.60), channel_id=1, source_target_pairs={{0,8},{8,16},{16,24},{24,0},{1,9},{9,17},{17,25},{25,1},{2,10},{10... | collective-permute-start | bytes 884744 | tf_op jit(solution)/shard_map/ppermute | solution.py:176
  363.3 19.1 %collective-permute-start.29 = (bf16[192,768]{1,0:T(8,128)(2,1)S(1)}, bf16[192,768]{1,0:T(8,128)(2,1)S(1)}, u32[]{:S(2)}, u32[]{:S(2)}) collective-permute-start(bf16[192,768]{1,0:T(8,128)(2,1)S(1)} %get-tuple-element.61), channel_id=1, source_target_pairs={{0,16},{8,24},{16,0},{24,8},{1,17},{9,25},{17,1},{25,9},{2,18},{10... | collective-permute-start | bytes 884744 | tf_op jit(solution)/shard_map/ppermute | solution.py:176
  367.7 17.9 %collective-permute-start.30 = (bf16[192,768]{1,0:T(8,128)(2,1)S(1)}, bf16[192,768]{1,0:T(8,128)(2,1)S(1)}, u32[]{:S(2)}, u32[]{:S(2)}) collective-permute-start(bf16[192,768]{1,0:T(8,128)(2,1)S(1)} %get-tuple-element.62), channel_id=1, source_target_pairs={{0,24},{8,0},{16,8},{24,16},{1,25},{9,1},{17,9},{25,17},{2,26},{10... | collective-permute-start | bytes 884744 | tf_op jit(solution)/shard_map/ppermute | solution.py:176
  415.6 32.1 %collective-permute-start.45 = (bf16[768,768]{1,0:T(8,128)(2,1)S(1)}, bf16[768,768]{1,0:T(8,128)(2,1)S(1)}, u32[]{:S(2)}, u32[]{:S(2)}) collective-permute-start(bf16[768,768]{1,0:T(8,128)(2,1)S(1)} %constant_dynamic-update-slice_fusion.14), channel_id=1, source_target_pairs={{0,96},{32,0},{64,32},{96,64},{1,97},{33,1},{65,33},{97,65},{2,98}... | collective-permute-start | bytes 3538952 | tf_op jit(solution)/shard_map/ppermute | solution.py:176
  421.1 29.6 %collective-permute-start.44 = (bf16[768,768]{1,0:T(8,128)(2,1)S(1)}, bf16[768,768]{1,0:T(8,128)(2,1)S(1)}, u32[]{:S(2)}, u32[]{:S(2)}) collective-permute-start(bf16[768,768]{1,0:T(8,128)(2,1)S(1)} %constant_dynamic-update-slice_fusion.14), channel_id=1, source_target_pairs={{0,32},{32,64},{64,96},{96,0},{1,33},{33,65},{65,97},{97,1},{2,34}... | collective-permute-start | bytes 3538952 | tf_op jit(solution)/shard_map/ppermute | solution.py:176
  (107 other events, 1011.1 us)

commit v4 on v1

--- a/solution.py
+++ b/solution.py
@@ -63,10 +63,10 @@
     for h in range(q_ref.shape[1] // HDIM):
         cols = slice(h * HDIM, (h + 1) * HDIM)
         raw = lax.dot_general(
-            q_ref[:, cols], k_ref[:, cols], (((1,), (1,)), ((), ())),
+            q_ref[:, cols] * scale, k_ref[:, cols], (((1,), (1,)), ((), ())),
             preferred_element_type=jnp.float32,
         )
-        scores = jnp.where(allowed, raw * scale, -1e30)
+        scores = jnp.where(allowed, raw, -1e30)
         highest = jnp.max(scores, axis=1, keepdims=True)
         expd = jnp.exp(scores - highest)
         total = jnp.sum(expd, axis=1, keepdims=True)
@@ -89,8 +89,8 @@
         k = k_ref[:, cols]
         v = v_ref[:, cols]
         do = do_ref[:, cols]
-        raw = lax.dot_general(q, k, (((1,), (1,)), ((), ())), preferred_element_type=jnp.float32)
-        scores = jnp.where(allowed, raw * scale, -1e30)
+        raw = lax.dot_general(q * scale, k, (((1,), (1,)), ((), ())), preferred_element_type=jnp.float32)
+        scores = jnp.where(allowed, raw, -1e30)
         probs = jnp.exp(scores - lse_ref[:, h:h + 1])
         grad_probs = lax.dot_general(do, v, (((1,), (1,)), ((), ())), preferred_element_type=jnp.float32)
         inner = jnp.sum(probs * grad_probs, axis=1, keepdims=True)

time: 481 us -> 481 us (level)
  no operation moved by 1% of the time
where the time goes in v4:
time: 481 us; the launch traced here: 473 us
  waiting for transfers between devices  120 us (25%)
  local copies, waits for them, and re-layouts  77.6 us (16%)
  starting transfers between devices  75.6 us (16%)
  matrix products  72.3 us (15%)
  other arithmetic  69.2 us (14%)
  Pallas kernels  55.1 us (11%)
    ppermute x32, waiting for transfers between devices, shift(): return lax.ppermute(x, axis, [(i, (i + step) % n) for i in range(n)])  79.1 us
    ppermute x32, starting transfers between devices, shift(): return lax.ppermute(x, axis, [(i, (i + step) % n) for i in range(n)])  53.4 us
    pallas_call x1, Pallas kernels, attention_backward(): pl.pallas_call(attention_backward_kernel, grid=(pairs,), in_specs=[pl.Blo...  31 us
    dot_general x7, matrix products, matmul(): return jnp.dot(left, right, preferred_element_type=jnp.float32)  30.1 us
    dot_general x13, matrix products, contract_rows(): lax.dot_general(left, right, (((0,), (0,)), ((), ())), preferred_element_...  24.2 us
    pallas_call x1, Pallas kernels, attention_forward(): pl.pallas_call(attention_forward_kernel, grid=(pairs,), in_specs=[pl.Bloc...  24.1 us
    dot_general x7, matrix products, contract_cols(): lax.dot_general(left, right, (((1,), (1,)), ((), ())), preferred_element_...  18.1 us
    ppermute x1, waiting for transfers between devices, from_sequence(): second = lax.ppermute(second, GRP, [(2, 0), (0, 1), (3, 2), (1, 3)])  15.6 us
  transfers between devices with their start and end apart: 48, of which 19 were waited for; matrix products, arithmetic and copies ran while one was open for 22% of the time, Pallas kernels for 5%

profile of v4, /device:TPU:0, one launch (start us, length us, event | category | flops | bytes accessed | tf_op | source)
XLA Modules:
  0.0 472.7 jit_solution(8854881105045776120)
XLA Ops:
  28.3 9.0 %collective-permute-done.8 = bf16[240,768]{1,0:T(8,128)(2,1)} collective-permute-done((bf16[240,768]{1,0:T(8,128)(2,1)}, bf16[240,768]{1,0:T(8,128)(2,1)}, u32[]{:S(2)}, u32[]{:S(2)}) %collective-permute-start.8) | collective-permute-done | bytes 368672 | tf_op jit(solution)/shard_map/ppermute | solution.py:248
  103.3 24.1 %shard_map.178 = (f32[512,768]{1,0:T(8,128)}, f32[6,512,2]{2,1,0:T(8,128)}) custom-call(bf16[512,768]{1,0:T(8,128)(2,1)} %copy.27.q_ref, bf16[1024,1536]{1,0:T(8,128)(2,1)} %pad_maximum_fusion.2.k_ref.v_ref, bf16[1024,1536]{1,0:T(8,128)(2,1)} %pad_maximum_fusion.2.k_ref.v_ref, s32[512,1]{1,0:T(8,128)} %iota_add_fusion.rq_ref, s32[512,1]{1,0:T(8,128)} %copy.28.sq_ref, ...), custom_call_target="tpu_custom_call" | custom-call | flops 1610612736 | bytes 5505024 | tf_op jit(solution)/shard_map/pallas_call | solution.py:118
  134.5 8.0 %fusion.20 = f32[512,3072]{1,0:T(8,128)} fusion(bf16[1536,768]{1,0:T(8,128)(2,1)S(1)} %get-tuple-element.119, bf16[1536,768]{1,0:T(8,128)(2,1)S(1)} %get-tuple-element.118, pred[]{:T(512)S(6)} %eq.70, bf16[512,1536]{1,0:T(8,128)(2,1)S(1)} %maximum_select_fusion.7), kind=kOutput, calls=%fused_computation.131 | convolution fusion | flops 2437152768 | bytes 11796481 | tf_op jit(solution)/shard_map/dot_general | solution.py:45
  152.2 4.7 fusion.23
  156.9 12.4 %multiply_convert_fusion.1 = (bf16[512,3072]{1,0:T(8,128)(2,1)}, bf16[512,3072]{1,0:T(8,128)(2,1)}, bf16[512,3072]{1,0:T(8,128)(2,1)}) fusion(f32[512,3072]{1,0:T(8,128)} %fusion.23, f32[512,3072]{1,0:T(8,128)} %fusion.20, bf16[512,768]{1,0:T(8,128)(2,1)S(1)} %multiply_convert_fusion.2, bf16[384,3072]{1,0:T(8,128)(2,1)S(1)} %copy-done.31, ...), kind=kOutput, calls=%fused_computation.5 | convolution fusion | flops 2465464320 | bytes 27525120 | tf_op jit(solution)/shard_map/dot_general | solution.py:35
  186.6 31.0 %shard_map.179 = (f32[512,768]{1,0:T(8,128)}, f32[1024,768]{1,0:T(8,128)}, f32[1024,768]{1,0:T(8,128)}) custom-call(bf16[512,768]{1,0:T(8,128)(2,1)} %copy.27.q_ref, bf16[1024,1536]{1,0:T(8,128)(2,1)} %pad_maximum_fusion.2.k_ref.v_ref, bf16[1024,1536]{1,0:T(8,128)(2,1)} %pad_maximum_fusion.2.k_ref.v_ref, bf16[512,768]{1,0:T(8,128)(2,1)} %convolution_convert_fusion.13.do_ref, ...), custom_call_target="tpu_custom_call" | custom-call | flops 4026531840 | bytes 12582912 | tf_op jit(solution)/shard_map/pallas_call | solution.py:147
  240.2 4.5 convolution_convert_fusion
  261.2 6.5 %constant_dynamic-slice_fusion.3 = (bf16[1,3072,768]{2,1,0:T(8,128)(2,1)}, bf16[1,3072,768]{2,1,0:T(8,128)(2,1)}, bf16[1,3072,768]{2,1,0:T(8,128)(2,1)}, bf16[1,3072,768]{2,1,0:T(8,128)(2,1)}) fusion(bf16[4,3072,768]{2,1,0:T(8,128)(2,1)S(1)} %constant_dynamic-update-slice_fusion.4, s32[]{:T(128)S(6)} %select_n.453, s32[]{:T(128)S(6)} %select_n.456, ...), kind=kLoop, calls=%fused_computation.251 | loop fusion | bytes 37748752 | tf_op jit(solution)/shard_map/jit(dynamic_index_in_dim)/dynamic_slice | solution.py:296
  267.7 8.4 %pad_maximum_fusion = bf16[2,3072,768]{2,1,0:T(8,128)(2,1)} fusion(bf16[1,3072,768]{2,1,0:T(8,128)(2,1)} %get-tuple-element.28, bf16[1,3072,768]{2,1,0:T(8,128)(2,1)} %get-tuple-element.29), kind=kLoop, calls=%fused_computation.1 | loop fusion | flops 4718592 | bytes 18874368 | tf_op jit(solution)/shard_map/stack | solution.py:298
  276.4 8.2 %add_convert_fusion.2 = bf16[512,768]{1,0:T(8,128)(2,1)} fusion(f32[512,768]{1,0:T(8,128)S(1)} %copy-done.5, bf16[512,3072]{1,0:T(8,128)(2,1)} %get-tuple-element.31, bf16[1536,768]{1,0:T(8,128)(2,1)} %copy-done.27, bf16[1536,768]{1,0:T(8,128)(2,1)} %copy-done.26, pred[]{:T(512)S(6)} %eq.70), kind=kOutput, calls=%fused_computation.73 | convolution fusion | flops 2437939200 | bytes 10223617 | tf_op jit(solution)/shard_map/dot_general | solution.py:35
  284.5 6.6 %collective-permute-done.23 = bf16[2,3072,768]{2,1,0:T(8,128)(2,1)} collective-permute-done((bf16[2,3072,768]{2,1,0:T(8,128)(2,1)}, bf16[2,3072,768]{2,1,0:T(8,128)(2,1)}, u32[]{:S(2)}, u32[]{:S(2)}) %collective-permute-start.23) | collective-permute-done | bytes 9437216 | tf_op jit(solution)/shard_map/ppermute | solution.py:252
  291.1 7.5 %convert_add_fusion = f32[2,3072,768]{2,1,0:T(8,128)S(1)} fusion(bf16[2,3072,768]{2,1,0:T(8,128)(2,1)} %collective-permute-done.23, bf16[1,3072,768]{2,1,0:T(8,128)(2,1)} %get-tuple-element.30, bf16[1,3072,768]{2,1,0:T(8,128)(2,1)} %get-tuple-element.27), kind=kLoop, calls=%fused_computation | loop fusion | flops 18874368 | bytes 37748736 | tf_op jit(solution)/shard_map/add | solution.py:299
  298.6 7.0 %fusion.101 = (f32[1,3072,768]{2,1,0:T(8,128)}, f32[1,3072,768]{2,1,0:T(8,128)}) fusion(f32[2,3072,768]{2,1,0:T(8,128)S(1)} %convert_add_fusion), kind=kLoop, calls=%fused_computation.296 | loop fusion | bytes 37748736 | tf_op jit(solution)/shard_map/slice | solution.py:302
  321.9 21.2 %collective-permute-done.32 = bf16[2,4,192,384]{3,2,1,0:T(8,128)(2,1)S(1)} collective-permute-done((bf16[2,4,192,384]{3,2,1,0:T(8,128)(2,1)S(1)}, bf16[2,4,192,384]{3,2,1,0:T(8,128)(2,1)S(1)}, u32[]{:S(2)}, u32[]{:S(2)}) %collective-permute-start.32) | collective-permute-done | bytes 1179680 | tf_op jit(solution)/shard_map/ppermute | solution.py:176
  347.8 11.4 %collective-permute-done.35 = bf16[4,192,384]{2,1,0:T(8,128)(2,1)S(1)} collective-permute-done((bf16[4,192,384]{2,1,0:T(8,128)(2,1)S(1)}, bf16[4,192,384]{2,1,0:T(8,128)(2,1)S(1)}, u32[]{:S(2)}, u32[]{:S(2)}) %collective-permute-start.35) | collective-permute-done | bytes 589856 | tf_op jit(solution)/shard_map/ppermute | solution.py:176
  363.7 4.4 collective-permute-start.29
  368.1 9.6 %collective-permute-done.34 = bf16[4,192,384]{2,1,0:T(8,128)(2,1)S(1)} collective-permute-done((bf16[4,192,384]{2,1,0:T(8,128)(2,1)S(1)}, bf16[4,192,384]{2,1,0:T(8,128)(2,1)S(1)}, u32[]{:S(2)}, u32[]{:S(2)}) %collective-permute-start.34) | collective-permute-done | bytes 589856 | tf_op jit(solution)/shard_map/ppermute | solution.py:176
  378.0 4.5 collective-permute-start.37
  395.8 5.4 %collective-permute-done.40 = bf16[192,768]{1,0:T(8,128)(2,1)S(1)} collective-permute-done((bf16[192,768]{1,0:T(8,128)(2,1)S(1)}, bf16[192,768]{1,0:T(8,128)(2,1)S(1)}, u32[]{:S(2)}, u32[]{:S(2)}) %collective-permute-start.40) | collective-permute-done | bytes 294944 | tf_op jit(solution)/shard_map/ppermute | solution.py:312
  409.2 6.6 %collective-permute-done.41 = bf16[192,768]{1,0:T(8,128)(2,1)S(1)} collective-permute-done((bf16[192,768]{1,0:T(8,128)(2,1)S(1)}, bf16[192,768]{1,0:T(8,128)(2,1)S(1)}, u32[]{:S(2)}, u32[]{:S(2)}) %collective-permute-start.41) | collective-permute-done | bytes 294944 | tf_op jit(solution)/shard_map/ppermute | solution.py:176
  415.9 5.6 %collective-permute-start.45 = (bf16[768,768]{1,0:T(8,128)(2,1)S(1)}, bf16[768,768]{1,0:T(8,128)(2,1)S(1)}, u32[]{:S(2)}, u32[]{:S(2)}) collective-permute-start(bf16[768,768]{1,0:T(8,128)(2,1)S(1)} %constant_dynamic-update-slice_fusion.14), channel_id=1, source_target_pairs={{0,96},{32,0},{64,32},{96,64},{1,97},{33,1},{65,33},{97,65},{2,98}... | collective-permute-start | bytes 3538952 | tf_op jit(solution)/shard_map/ppermute | solution.py:176
  422.9 7.4 %collective-permute-start.21 = (bf16[256,1536]{1,0:T(8,128)(2,1)}, bf16[256,1536]{1,0:T(8,128)(2,1)}, u32[]{:S(2)}, u32[]{:S(2)}) collective-permute-start(bf16[256,1536]{1,0:T(8,128)(2,1)} %get-tuple-element.86), channel_id=1, source_target_pairs={{0,0},{1,2},{2,1},{3,3},{4,4},{5,6},{6,5},{7,7},{8,8},{9,10},{10,9... | collective-permute-start | bytes 2359304 | tf_op jit(solution)/shard_map/ppermute | solution.py:339
  430.4 15.6 %collective-permute-done.22 = bf16[256,1536]{1,0:T(8,128)(2,1)} collective-permute-done((bf16[256,1536]{1,0:T(8,128)(2,1)}, bf16[256,1536]{1,0:T(8,128)(2,1)}, u32[]{:S(2)}, u32[]{:S(2)}) %collective-permute-start.22) | collective-permute-done | bytes 786464 | tf_op jit(solution)/shard_map/ppermute | solution.py:340
  453.1 8.6 %collective-permute-done.47 = bf16[384,768]{1,0:T(8,128)(2,1)S(1)} collective-permute-done((bf16[384,768]{1,0:T(8,128)(2,1)S(1)}, bf16[384,768]{1,0:T(8,128)(2,1)S(1)}, u32[]{:S(2)}, u32[]{:S(2)}) %collective-permute-start.47) | collective-permute-done | bytes 589856 | tf_op jit(solution)/shard_map/ppermute | solution.py:176
  (415 shorter events, 232.0 us)
Async XLA Ops:
  2.6 23.0 %collective-permute-start.2 = (bf16[144,768]{1,0:T(8,128)(2,1)}, bf16[144,768]{1,0:T(8,128)(2,1)}, u32[]{:S(2)}, u32[]{:S(2)}) collective-permute-start(bf16[144,768]{1,0:T(8,128)(2,1)} %fusion.68), channel_id=1, source_target_pairs={{0,6},{2,4},{4,2},{6,0},{1,7},{3,5},{5,3},{7,1},{8,14},{10,12},{12... | collective-permute-start | bytes 663560 | tf_op jit(solution)/shard_map/ppermute | solution.py:248
  7.4 29.9 %collective-permute-start.8 = (bf16[240,768]{1,0:T(8,128)(2,1)}, bf16[240,768]{1,0:T(8,128)(2,1)}, u32[]{:S(2)}, u32[]{:S(2)}) collective-permute-start(bf16[240,768]{1,0:T(8,128)(2,1)} %fusion.65), channel_id=1, source_target_pairs={{0,6},{2,4},{4,2},{6,0},{1,7},{3,5},{5,3},{7,1},{8,14},{10,12},{12... | collective-permute-start | bytes 1105928 | tf_op jit(solution)/shard_map/ppermute | solution.py:248
  8.9 41.1 %collective-permute-start.14 = (bf16[96,3072]{1,0:T(8,128)(2,1)}, bf16[96,3072]{1,0:T(8,128)(2,1)}, u32[]{:S(2)}, u32[]{:S(2)}) collective-permute-start(bf16[96,3072]{1,0:T(8,128)(2,1)} %fusion.39), channel_id=1, source_target_pairs={{0,6},{2,4},{4,2},{6,0},{1,7},{3,5},{5,3},{7,1},{8,14},{10,12},{12... | collective-permute-start | bytes 1769480 | tf_op jit(solution)/shard_map/ppermute | solution.py:248
  14.0 45.7 %collective-permute-start = (bf16[256,1536]{1,0:T(8,128)(2,1)}, bf16[256,1536]{1,0:T(8,128)(2,1)S(1)}, u32[]{:S(2)}, u32[]{:S(2)}) collective-permute-start(bf16[256,1536]{1,0:T(8,128)(2,1)} %get-tuple-element.88), channel_id=1, source_target_pairs={{0,0},{1,2},{2,1},{3,3},{4,4},{5,6},{6,5},{7,7},{8,8},{9,10},{10,9... | collective-permute-start | bytes 2359304 | tf_op jit(solution)/shard_map/ppermute | solution.py:328
  15.8 45.5 %collective-permute-start.1 = (bf16[256,1536]{1,0:T(8,128)(2,1)S(1)}, bf16[256,1536]{1,0:T(8,128)(2,1)S(1)}, u32[]{:S(2)}, u32[]{:S(2)}) collective-permute-start(bf16[256,1536]{1,0:T(8,128)(2,1)S(1)} %get-tuple-element.89), channel_id=1, source_target_pairs={{0,2},{1,0},{2,3},{3,1},{4,6},{5,4},{6,7},{7,5},{8,10},{9,8},{10,1... | collective-permute-start | bytes 2359304 | tf_op jit(solution)/shard_map/ppermute | solution.py:329
  25.7 16.0 %collective-permute-start.3 = (bf16[144,768]{1,0:T(8,128)(2,1)}, bf16[144,768]{1,0:T(8,128)(2,1)S(1)}, u32[]{:S(2)}, u32[]{:S(2)}) collective-permute-start(bf16[144,768]{1,0:T(8,128)(2,1)} %collective-permute-done.2), channel_id=1, source_target_pairs={{0,32},{32,64},{64,96},{96,0},{1,33},{33,65},{65,97},{97,1},{2,34}... | collective-permute-start | bytes 663560 | tf_op jit(solution)/shard_map/ppermute | solution.py:176
  50.0 27.9 %collective-permute-start.6 = (bf16[1152,768]{1,0:T(8,128)(2,1)S(1)}, bf16[1152,768]{1,0:T(8,128)(2,1)S(1)}, u32[]{:S(2)}, u32[]{:S(2)}) collective-permute-start(bf16[1152,768]{1,0:T(8,128)(2,1)S(1)} %pad_maximum_fusion.6), channel_id=1, source_target_pairs={{0,1},{1,0},{2,3},{3,2},{4,5},{5,4},{6,7},{7,6},{8,9},{9,8},{10,11... | collective-permute-start | bytes 5308424 | tf_op jit(solution)/shard_map/ppermute | solution.py:252
  54.3 18.3 %collective-permute-start.16 = (bf16[96,3072]{1,0:T(8,128)(2,1)}, bf16[96,3072]{1,0:T(8,128)(2,1)S(1)}, u32[]{:S(2)}, u32[]{:S(2)}) collective-permute-start(bf16[96,3072]{1,0:T(8,128)(2,1)} %collective-permute-done.14), channel_id=1, source_target_pairs={{0,96},{32,0},{64,32},{96,64},{1,97},{33,1},{65,33},{97,65},{2,98}... | collective-permute-start | bytes 1769480 | tf_op jit(solution)/shard_map/ppermute | solution.py:176
  58.0 18.6 %collective-permute-start.15 = (bf16[96,3072]{1,0:T(8,128)(2,1)}, bf16[96,3072]{1,0:T(8,128)(2,1)S(1)}, u32[]{:S(2)}, u32[]{:S(2)}) collective-permute-start(bf16[96,3072]{1,0:T(8,128)(2,1)} %collective-permute-done.14), channel_id=1, source_target_pairs={{0,32},{32,64},{64,96},{96,0},{1,33},{33,65},{65,97},{97,1},{2,34}... | collective-permute-start | bytes 1769480 | tf_op jit(solution)/shard_map/ppermute | solution.py:176
  72.6 54.8 %collective-permute-start.13 = (bf16[1920,768]{1,0:T(8,128)(2,1)}, bf16[1920,768]{1,0:T(8,128)(2,1)}, u32[]{:S(2)}, u32[]{:S(2)}) collective-permute-start(bf16[1920,768]{1,0:T(8,128)(2,1)} %pad_maximum_fusion.3), channel_id=1, source_target_pairs={{0,1},{1,0},{2,3},{3,2},{4,5},{5,4},{6,7},{7,6},{8,9},{9,8},{10,11... | collective-permute-start | bytes 8847368 | tf_op jit(solution)/shard_map/ppermute | solution.py:252
  73.4 17.8 %collective-permute-start.18 = (bf16[48,3072]{1,0:T(8,128)(2,1)}, bf16[48,3072]{1,0:T(8,128)(2,1)}, u32[]{:S(2)}, u32[]{:S(2)}) collective-permute-start(bf16[48,3072]{1,0:T(8,128)(2,1)} %slice.395), channel_id=1, source_target_pairs={{0,96},{32,0},{64,32},{96,64},{1,97},{33,1},{65,33},{97,65},{2,98}... | collective-permute-start | bytes 884744 | tf_op jit(solution)/shard_map/ppermute | solution.py:176
  94.7 47.8 %collective-permute-start.19 = (bf16[768,3072]{1,0:T(8,128)(2,1)}, bf16[768,3072]{1,0:T(8,128)(2,1)}, u32[]{:S(2)}, u32[]{:S(2)}) collective-permute-start(bf16[768,3072]{1,0:T(8,128)(2,1)} %pad_maximum_fusion.1), channel_id=1, source_target_pairs={{0,1},{1,0},{2,3},{3,2},{4,5},{5,4},{6,7},{7,6},{8,9},{9,8},{10,11... | collective-permute-start | bytes 14155784 | tf_op jit(solution)/shard_map/ppermute | solution.py:252
  224.1 20.6 %collective-permute-start.20 = (f32[512,1536]{1,0:T(8,128)S(1)}, f32[512,1536]{1,0:T(8,128)S(1)}, u32[]{:S(2)}, u32[]{:S(2)}) collective-permute-start(f32[512,1536]{1,0:T(8,128)S(1)} %slice.409), channel_id=1, source_target_pairs={{0,1},{1,0},{2,3},{3,2},{4,5},{5,4},{6,7},{7,6},{8,9},{9,8},{10,11... | collective-permute-start | bytes 9437192 | tf_op jit(solution)/shard_map/ppermute | solution.py:252
  313.7 29.4 %collective-permute-start.32 = (bf16[2,4,192,384]{3,2,1,0:T(8,128)(2,1)S(1)}, bf16[2,4,192,384]{3,2,1,0:T(8,128)(2,1)S(1)}, u32[]{:S(2)}, u32[]{:S(2)}) collective-permute-start(bf16[2,4,192,384]{3,2,1,0:T(8,128)(2,1)S(1)} %pad_maximum_fusion.10), channel_id=1, source_target_pairs={{0,8},{8,16},{16,24},{24,0},{1,9},{9,17},{17,25},{25,1},{2,10},{10... | collective-permute-start | bytes 3538952 | tf_op jit(solution)/shard_map/ppermute | solution.py:176
  313.9 30.3 %collective-permute-start.25 = (bf16[2,768,384]{2,1,0:T(8,128)(2,1)S(1)}, bf16[2,768,384]{2,1,0:T(8,128)(2,1)S(1)}, u32[]{:S(2)}, u32[]{:S(2)}) collective-permute-start(bf16[2,768,384]{2,1,0:T(8,128)(2,1)S(1)} %pad_maximum_fusion.9), channel_id=1, source_target_pairs={{0,96},{32,0},{64,32},{96,64},{1,97},{33,1},{65,33},{97,65},{2,98}... | collective-permute-start | bytes 3538952 | tf_op jit(solution)/shard_map/ppermute | solution.py:176
  317.5 30.0 %collective-permute-start.24 = (bf16[2,768,384]{2,1,0:T(8,128)(2,1)S(1)}, bf16[2,768,384]{2,1,0:T(8,128)(2,1)S(1)}, u32[]{:S(2)}, u32[]{:S(2)}) collective-permute-start(bf16[2,768,384]{2,1,0:T(8,128)(2,1)S(1)} %pad_maximum_fusion.8), channel_id=1, source_target_pairs={{0,32},{32,64},{64,96},{96,0},{1,33},{33,65},{65,97},{97,1},{2,34}... | collective-permute-start | bytes 3538952 | tf_op jit(solution)/shard_map/ppermute | solution.py:176
  317.7 30.0 %collective-permute-start.33 = (bf16[2,4,192,384]{3,2,1,0:T(8,128)(2,1)S(1)}, bf16[2,4,192,384]{3,2,1,0:T(8,128)(2,1)S(1)}, u32[]{:S(2)}, u32[]{:S(2)}) collective-permute-start(bf16[2,4,192,384]{3,2,1,0:T(8,128)(2,1)S(1)} %pad_maximum_fusion.11), channel_id=1, source_target_pairs={{0,24},{8,0},{16,8},{24,16},{1,25},{9,1},{17,9},{25,17},{2,26},{10... | collective-permute-start | bytes 3538952 | tf_op jit(solution)/shard_map/ppermute | solution.py:176
  344.3 16.5 %collective-permute-start.26 = (bf16[768,384]{1,0:T(8,128)(2,1)S(1)}, bf16[768,384]{1,0:T(8,128)(2,1)S(1)}, u32[]{:S(2)}, u32[]{:S(2)}) collective-permute-start(bf16[768,384]{1,0:T(8,128)(2,1)S(1)} %fusion.17), channel_id=1, source_target_pairs={{0,96},{32,0},{64,32},{96,64},{1,97},{33,1},{65,33},{97,65},{2,98}... | collective-permute-start | bytes 1769480 | tf_op jit(solution)/shard_map/ppermute | solution.py:176
  359.5 18.2 %collective-permute-start.34 = (bf16[4,192,384]{2,1,0:T(8,128)(2,1)S(1)}, bf16[4,192,384]{2,1,0:T(8,128)(2,1)S(1)}, u32[]{:S(2)}, u32[]{:S(2)}) collective-permute-start(bf16[4,192,384]{2,1,0:T(8,128)(2,1)S(1)} %get-tuple-element.35), channel_id=1, source_target_pairs={{0,24},{8,0},{16,8},{24,16},{1,25},{9,1},{17,9},{25,17},{2,26},{10... | collective-permute-start | bytes 1769480 | tf_op jit(solution)/shard_map/ppermute | solution.py:176
  363.6 18.9 %collective-permute-start.28 = (bf16[192,768]{1,0:T(8,128)(2,1)S(1)}, bf16[192,768]{1,0:T(8,128)(2,1)S(1)}, u32[]{:S(2)}, u32[]{:S(2)}) collective-permute-start(bf16[192,768]{1,0:T(8,128)(2,1)S(1)} %get-tuple-element.60), channel_id=1, source_target_pairs={{0,8},{8,16},{16,24},{24,0},{1,9},{9,17},{17,25},{25,1},{2,10},{10... | collective-permute-start | bytes 884744 | tf_op jit(solution)/shard_map/ppermute | solution.py:176
  363.7 19.1 %collective-permute-start.29 = (bf16[192,768]{1,0:T(8,128)(2,1)S(1)}, bf16[192,768]{1,0:T(8,128)(2,1)S(1)}, u32[]{:S(2)}, u32[]{:S(2)}) collective-permute-start(bf16[192,768]{1,0:T(8,128)(2,1)S(1)} %get-tuple-element.61), channel_id=1, source_target_pairs={{0,16},{8,24},{16,0},{24,8},{1,17},{9,25},{17,1},{25,9},{2,18},{10... | collective-permute-start | bytes 884744 | tf_op jit(solution)/shard_map/ppermute | solution.py:176
  368.1 17.9 %collective-permute-start.30 = (bf16[192,768]{1,0:T(8,128)(2,1)S(1)}, bf16[192,768]{1,0:T(8,128)(2,1)S(1)}, u32[]{:S(2)}, u32[]{:S(2)}) collective-permute-start(bf16[192,768]{1,0:T(8,128)(2,1)S(1)} %get-tuple-element.62), channel_id=1, source_target_pairs={{0,24},{8,0},{16,8},{24,16},{1,25},{9,1},{17,9},{25,17},{2,26},{10... | collective-permute-start | bytes 884744 | tf_op jit(solution)/shard_map/ppermute | solution.py:176
  415.9 32.1 %collective-permute-start.45 = (bf16[768,768]{1,0:T(8,128)(2,1)S(1)}, bf16[768,768]{1,0:T(8,128)(2,1)S(1)}, u32[]{:S(2)}, u32[]{:S(2)}) collective-permute-start(bf16[768,768]{1,0:T(8,128)(2,1)S(1)} %constant_dynamic-update-slice_fusion.14), channel_id=1, source_target_pairs={{0,96},{32,0},{64,32},{96,64},{1,97},{33,1},{65,33},{97,65},{2,98}... | collective-permute-start | bytes 3538952 | tf_op jit(solution)/shard_map/ppermute | solution.py:176
  421.5 29.6 %collective-permute-start.44 = (bf16[768,768]{1,0:T(8,128)(2,1)S(1)}, bf16[768,768]{1,0:T(8,128)(2,1)S(1)}, u32[]{:S(2)}, u32[]{:S(2)}) collective-permute-start(bf16[768,768]{1,0:T(8,128)(2,1)S(1)} %constant_dynamic-update-slice_fusion.14), channel_id=1, source_target_pairs={{0,32},{32,64},{64,96},{96,0},{1,33},{33,65},{65,97},{97,1},{2,34}... | collective-permute-start | bytes 3538952 | tf_op jit(solution)/shard_map/ppermute | solution.py:176
  (107 other events, 1012.3 us)
